TPU v7x, 128 devices: a whole 4x4x4 slice. The times are simulated.
128 devices in a mesh: rows: 8 (over x_hi, z), samples: 4 (over x_lo, core), chan: 4 (over y).
Axes of the slice: x: 4 (x_hi: 2, x_lo: 2; x = x_hi * 2 + x_lo), y: 4, z: 4, core: 2. Of those that a mesh axis runs over, the one named last changes fastest.
Arguments:
- feature: bfloat16 [4, 256, 64, 512], P('samples', 'chan', 'rows'), may hold values from -6 to 6
- out_grad: bfloat16 [4, 256, 64, 512], P('samples', 'chan', 'rows'), may hold values from -6 to 6
- bank: float32 [4, 9, 256, 256], P(None, None, 'chan', 'rows'), may hold values from -0.125 to 0.125
- select: int32 [4, 4], P('samples'), may hold values from 1 to 8
- latent: float32 [4, 512], P('samples'), may hold values from -6 to 6
- affine_w: float32 [512, 256], P(None, 'rows'), may hold values from -0.25 to 0.25
- affine_b: float32 [256], P('rows'), may hold values from 0.5 to 1.5
Outputs:
- feature_grad: bfloat16 [4, 256, 64, 512], P('samples', 'chan', 'rows')
- bank_grad: float32 [4, 9, 256, 256], P(None, None, 'chan', 'rows')
- affine_w_grad: float32 [512, 256], P(None, 'rows')
- affine_b_grad: float32 [256], P('rows')
All inputs are finite; a program needn't handle non-finite values.
Results may differ from a plain program's by a relative error of at most 0.0049.
Values may be sent and summed in bfloat16 or wider, within the bound.
A program may use at most 128 MiB of HBM per device.

v0:
```python
import jax
import jax.numpy as jnp
from jax import lax
from jax.sharding import PartitionSpec as P

EPS = 1e-08


def extended(x, sides, width):
    for axis, dim in sides:
        size, length = (lax.axis_size(axis), x.shape[dim])
        up = [(i, (i + 1) % size) for i in range(size - 1)]
        down = [(j, i) for i, j in up]
        last = lax.slice_in_dim(x, length - width, length, axis=dim)
        leading = lax.slice_in_dim(x, 0, width, axis=dim)
        before = lax.ppermute(last, axis, up)
        after = lax.ppermute(leading, axis, down)
        x = jnp.concatenate([before, x, after], axis=dim)
    return x


def copy_for_each(x, axis):
    copies = jnp.broadcast_to(x, (lax.axis_size(axis), *x.shape))
    return lax.all_to_all(copies, axis, split_axis=0, concat_axis=0, tiled=True)


def taken_together(x, axis):
    everything = copy_for_each(x, axis)
    return jnp.sum(everything, axis=0)


def split_up(x, dim, size):
    lengths = x.shape
    parts = x.reshape(*lengths[:dim], size, lengths[dim] // size, *lengths[dim + 1 :])
    return jnp.moveaxis(parts, dim, 0)


def sent_and_summed(x, axis, dim):
    parts = split_up(x, dim, lax.axis_size(axis))
    arrived = lax.all_to_all(parts, axis, split_axis=0, concat_axis=0, tiled=True)
    return arrived.sum(axis=0)


def packed_total(arrays, axis):
    vector, at, outs = (jnp.concatenate([a.reshape(-1) for a in arrays]), 0, [])
    total = taken_together(vector, axis)
    for a in arrays:
        outs.append(total[at : at + a.size].reshape(a.shape))
        at += a.size
    return tuple(outs)


def tap_slice(padded, first_row, first_col, height, width):
    return padded[:, first_row : first_row + height, first_col : first_col + width].reshape(
        padded.shape[0], height * width
    )


def on_device(feature, out_grad, bank, select, latent, affine_w, affine_b):
    feat_own = feature[0]
    cotan_own = out_grad[0]
    local_ch = feat_own.shape[0]
    height = feat_own.shape[1]
    width = feat_own.shape[2]
    stacked = jnp.concatenate([feat_own, cotan_own], axis=0)
    rimmed = extended(stacked, (("rows", 1),), 1)
    feat_rim = rimmed[:local_ch]
    cotan_rim = rimmed[local_ch:]
    weights = select[0].astype(jnp.float32)
    kernel = jnp.einsum("k,ktoc->toc", weights, bank, precision=lax.Precision.HIGHEST)
    style = jnp.dot(latent, affine_w, precision=lax.Precision.HIGHEST)[0] + affine_b
    plain = kernel * style[None, None, :]
    energy = taken_together(jnp.sum(plain * plain, axis=(0, 2)), "rows")
    scale = lax.rsqrt(energy + EPS)
    modulated = (plain * scale[None, :, None]).astype(jnp.bfloat16)
    mod_rows = lax.all_gather(modulated, "rows", axis=2, tiled=True)
    cotan_flat = cotan_own.reshape(local_ch, height * width)
    piece_pad = jnp.pad(
        lax.all_gather(feat_rim, "chan", axis=0, tiled=True), ((0, 0), (0, 0), (1, 1))
    )
    grads = []
    for tap_index in range(9):
        feat_tap = tap_slice(piece_pad, tap_index // 3, tap_index % 3, height, width)
        grads.append(
            lax.dot_general(
                cotan_flat, feat_tap, (((1,), (1,)), ((), ())), preferred_element_type=jnp.float32
            )
        )
    grad_part = jnp.stack(grads, 0)
    mod_grad = sent_and_summed(grad_part, "rows", 2)
    mod_full = lax.all_gather(mod_rows, "chan", axis=1, tiled=True)
    own_first = lax.axis_index("chan") * local_ch
    mine = lax.dynamic_slice_in_dim(mod_full, own_first, local_ch, 2)
    empty = jnp.zeros((local_ch, height * width), jnp.float32)
    total = empty
    piece_pad = jnp.pad(
        lax.all_gather(cotan_rim, "chan", axis=0, tiled=True), ((0, 0), (0, 0), (1, 1))
    )
    for tap_index in range(9):
        cotan_tap = tap_slice(piece_pad, 2 - tap_index // 3, 2 - tap_index % 3, height, width)
        total = total + lax.dot_general(
            mine[tap_index], cotan_tap, (((0,), (0,)), ((), ())), preferred_element_type=jnp.float32
        )
    feature_grad = total.reshape(1, local_ch, height, width).astype(jnp.bfloat16)
    slope = taken_together(jnp.sum(mod_grad * plain, axis=(0, 2)), "rows")
    plain_grad = mod_grad * scale[None, :, None] - plain * (slope * scale**3)[None, :, None]
    kernel_grad = plain_grad * style[None, None, :]
    style_part = jnp.sum(plain_grad * kernel, axis=(0, 1))
    bank_part = weights[:, None, None, None] * kernel_grad[None]
    style_whole = lax.psum(style_part, "chan")
    affine_part = latent[0][:, None] * style_whole[None, :]
    bank_grad, affine_w_grad, affine_b_grad = packed_total(
        (bank_part, affine_part, style_whole), "samples"
    )
    return (feature_grad, bank_grad, affine_w_grad, affine_b_grad)


def solution(mesh):
    return jax.shard_map(
        on_device,
        mesh=mesh,
        in_specs=(
            P("samples", "chan", "rows", None),
            P("samples", "chan", "rows", None),
            P(None, None, "chan", "rows"),
            P("samples", None),
            P("samples", None),
            P(None, "rows"),
            P("rows"),
        ),
        out_specs=(
            P("samples", "chan", "rows", None),
            P(None, None, "chan", "rows"),
            P(None, "rows"),
            P("rows"),
        ),
        check_vma=False,
    )
```

profile of v0, /device:TPU:1, one launch (start us, length us, event | category | flops | bytes accessed | tf_op | source)
XLA Modules:
  0.0 250.4 jit_solution(1440929932458919679)
XLA Ops:
  8.8 4.4 %collective-permute-start = (bf16[128,1,512]{2,0,1:T(8,128)(2,1)S(1)}, bf16[128,1,512]{2,0,1:T(8,128)(2,1)S(1)}, u32[]{:S(2)}, u32[]{:S(2)}) collective-permute-start(bf16[128,1,512]{2,0,1:T(8,128)(2,1)S(1)} %get-tuple-element.50), channel_id=1, source_target_pairs={{0,16},{16,32},{32,48},{48,64},{64,80},{80,96},{96,112},{1,17},{17... | collective-permute-start | bytes 393224 | tf_op jit(solution)/shard_map/ppermute | solution.py:16
  15.4 4.2 %collective-permute-done.1 = bf16[128,1,512]{2,0,1:T(8,128)(2,1)S(1)} collective-permute-done((bf16[128,1,512]{2,0,1:T(8,128)(2,1)S(1)}, bf16[128,1,512]{2,0,1:T(8,128)(2,1)S(1)}, u32[]{:S(2)}, u32[]{:S(2)}) %collective-permute-start.1) | collective-permute-done | bytes 131104 | tf_op jit(solution)/shard_map/ppermute | solution.py:17
  21.6 38.5 %all-gather.8.cloned.1.call-done = bf16[256,10,512]{2,0,1:T(8,128)(2,1)} async-done(((bf16[64,10,512]{2,0,1:T(8,128)(2,1)}), bf16[256,10,512]{2,0,1:T(8,128)(2,1)}) %all-gather.8.cloned.1.call-update) | async-done | bytes 2621456 | tf_op jit(solution)/shard_map/all_gather | solution.py:79
  60.1 4.4 %copy.120 = bf16[256,10,512]{0,2,1:T(8,128)(2,1)} copy(bf16[256,10,512]{2,0,1:T(8,128)(2,1)} %all-gather.8.cloned.1.call-done) | data formatting | bytes 5242880 | tf_op jit(solution)/shard_map/all_gather | solution.py:79
  64.5 14.3 %pad_slice_fusion = (bf16[256,8,512]{0,2,1:T(8,128)(2,1)S(1)}, bf16[256,8,512]{0,2,1:T(8,128)(2,1)}, bf16[256,8,512]{0,2,1:T(8,128)(2,1)}, bf16[256,8,512]{0,2,1...) fusion(bf16[256,10,512]{0,2,1:T(8,128)(2,1)} %copy.120), kind=kLoop, calls=%fused_computation.10 | loop fusion | bytes 27787264 | tf_op jit(solution)/shard_map/slice | solution.py:54
  79.3 2.1 convolution_bitcast_fusion.7
  81.5 2.1 convolution_bitcast_fusion.6
  84.3 2.1 convolution_bitcast_fusion.5
  87.2 2.1 convolution_bitcast_fusion.4
  90.0 2.1 convolution_bitcast_fusion.3
  95.7 2.0 convolution_bitcast_fusion.1
  105.4 6.5 %all-to-all-start.1 = ((f32[8,1,18432]{2,1,0:T(1,128)}), f32[8,1,18432]{2,1,0:T(1,128)S(1)}, u32[]{:S(2)}, u32[]{:S(2)}) async-start(f32[8,1,18432]{2,1,0:T(1,128)} %reshape.180), calls=%async_computation.1 | async-start | bytes 1179648 | tf_op jit(solution)/shard_map/all_to_all | solution.py:40
  113.6 7.8 %all-to-all-done.1 = f32[8,1,18432]{2,1,0:T(1,128)S(1)} async-done(((f32[8,1,18432]{2,1,0:T(1,128)}), f32[8,1,18432]{2,1,0:T(1,128)S(1)}, u32[]{:S(2)}, u32[]{:S(2)}) %all-to-all-start.1) | async-done | bytes 589856 | tf_op jit(solution)/shard_map/all_to_all | solution.py:40
  124.7 12.1 %all_to_all.23 = f32[8,1,64]{2,1,0:T(1,128)S(1)} all-to-all(f32[8,1,64]{2,1,0:T(1,128)S(1)} %broadcast_in_dim.6), channel_id=1, replica_groups=mesh['rows'=8,'samples'=4,'chan'=4] {'rows'}, dimensions={0} | all-to-all | bytes 4096 | tf_op jit(solution)/shard_map/all_to_all | solution.py:24
  137.4 3.3 %all-to-all-start.2 = ((f32[8,1,64]{2,1,0:T(1,128)}), f32[8,1,64]{2,1,0:T(1,128)S(1)}, u32[]{:S(2)}, u32[]{:S(2)}) async-start(f32[8,1,64]{2,1,0:T(1,128)} %broadcast_in_dim.7), calls=%async_computation.2 | async-start | bytes 8192 | tf_op jit(solution)/shard_map/all_to_all | solution.py:24
  141.0 6.1 %all-to-all-done.2 = f32[8,1,64]{2,1,0:T(1,128)S(1)} async-done(((f32[8,1,64]{2,1,0:T(1,128)}), f32[8,1,64]{2,1,0:T(1,128)S(1)}, u32[]{:S(2)}, u32[]{:S(2)}) %all-to-all-start.2) | async-done | bytes 2080 | tf_op jit(solution)/shard_map/all_to_all | solution.py:24
  148.0 6.6 %psum.7 = f32[32]{0:T(128)S(1)} all-reduce(f32[32]{0:T(128)S(1)} %get-tuple-element.53), channel_id=1, replica_groups=mesh['rows'=8,'samples'=4,'chan'=4] {'chan'}, use_global_device_ids=true, to_apply=%region_6.7 | all-reduce | flops 32 | bytes 256 | tf_op jit(solution)/shard_map/psum | solution.py:110
  154.9 29.2 %all_gather.12 = bf16[9,64,256]{1,2,0:T(8,128)(2,1)S(1)} all-gather(bf16[9,64,32]{1,2,0:T(8,128)(2,1)S(1)} %get-tuple-element.54), channel_id=1, replica_groups=mesh['rows'=8,'samples'=4,'chan'=4] {'rows'}, dimensions={2}, use_global_device_ids=true | all-gather | bytes 331776 | tf_op jit(solution)/shard_map/all_gather | solution.py:76
  187.0 15.3 %all-to-all-start.3 = ((f32[4,1,90144]{2,1,0:T(1,128)}), f32[4,1,90144]{2,1,0:T(1,128)}, u32[]{:S(2)}, u32[]{:S(2)}) async-start(f32[4,1,90144]{2,1,0:T(1,128)} %broadcast_in_dim.8), calls=%async_computation.3 | async-start | bytes 2887680 | tf_op jit(solution)/shard_map/all_to_all | solution.py:24
  202.3 3.0 %copy.116 = bf16[256,10,512]{0,2,1:T(8,128)(2,1)S(1)} copy(bf16[256,10,512]{2,0,1:T(8,128)(2,1)} %all-gather.6.cloned.1.call-done) | data formatting | bytes 5242880 | tf_op jit(solution)/shard_map/all_gather | solution.py:97
  205.3 8.0 %pad_slice_fusion.6 = (bf16[256,8,512]{0,2,1:T(8,128)(2,1)}, bf16[256,8,512]{0,2,1:T(8,128)(2,1)}, bf16[256,8,512]{0,2,1:T(8,128)(2,1)}, bf16[256,8,512]{0,2,1:T...) fusion(bf16[256,10,512]{0,2,1:T(8,128)(2,1)S(1)} %copy.116), kind=kLoop, calls=%fused_computation.16 | loop fusion | bytes 27787264 | tf_op jit(solution)/shard_map/slice | solution.py:54
  213.2 6.9 %all-to-all-done.3 = f32[4,1,90144]{2,1,0:T(1,128)} async-done(((f32[4,1,90144]{2,1,0:T(1,128)}), f32[4,1,90144]{2,1,0:T(1,128)}, u32[]{:S(2)}, u32[]{:S(2)}) %all-to-all-start.3) | async-done | bytes 1442336 | tf_op jit(solution)/shard_map/all_to_all | solution.py:24
  220.1 2.7 %reduce_sum.69 = f32[90144]{0:T(1024)S(1)} reduce(f32[4,1,90144]{2,1,0:T(1,128)} %all-to-all-done.3, f32[]{:T(128)} %constant.2.clone.1), dimensions={0,1}, to_apply=%region_7.8 | reduce | flops 270432 | bytes 1802884 | tf_op jit(solution)/shard_map/reduce_sum | solution.py:29
  225.7 2.5 fusion.5
  (108 shorter events, 47.9 us)
Async XLA Ops:
  7.2 105.0 %copy-start = (f32[4,9,64,32]{2,3,1,0:T(8,128)S(1)}, f32[4,9,64,32]{2,3,1,0:T(8,128)}, u32[]{:S(2)}) copy-start(f32[4,9,64,32]{2,3,1,0:T(8,128)} %param.9) | copy-start | bytes 884740
  7.2 52.9 %all-gather.8.cloned.1.call-start = ((), (), s32[]{:S(2)}) async-start(), calls=%async_computation.6 | async-start | bytes 3276800 | tf_op jit(solution)/shard_map/all_gather | solution.py:79
  8.8 6.5 %collective-permute-start = (bf16[128,1,512]{2,0,1:T(8,128)(2,1)S(1)}, bf16[128,1,512]{2,0,1:T(8,128)(2,1)S(1)}, u32[]{:S(2)}, u32[]{:S(2)}) collective-permute-start(bf16[128,1,512]{2,0,1:T(8,128)(2,1)S(1)} %get-tuple-element.50), channel_id=1, source_target_pairs={{0,16},{16,32},{32,48},{48,64},{64,80},{80,96},{96,112},{1,17},{17... | collective-permute-start | bytes 393224 | tf_op jit(solution)/shard_map/ppermute | solution.py:16
  13.2 6.4 %collective-permute-start.1 = (bf16[128,1,512]{2,0,1:T(8,128)(2,1)S(1)}, bf16[128,1,512]{2,0,1:T(8,128)(2,1)S(1)}, u32[]{:S(2)}, u32[]{:S(2)}) collective-permute-start(bf16[128,1,512]{2,0,1:T(8,128)(2,1)S(1)} %get-tuple-element.51), channel_id=1, source_target_pairs={{16,0},{32,16},{48,32},{64,48},{80,64},{96,80},{112,96},{17,1},{33... | collective-permute-start | bytes 393224 | tf_op jit(solution)/shard_map/ppermute | solution.py:17
  19.6 1.3 copy-start.10
  20.8 181.4 %all-gather.6.cloned.1.call-start = ((), (), s32[]{:S(2)}) async-start(), calls=%async_computation.5 | async-start | bytes 3276800 | tf_op jit(solution)/shard_map/all_gather | solution.py:97
  98.9 4.7 %copy-start.11 = (f32[64,256]{0,1:T(8,128)S(1)}, f32[64,256]{0,1:T(8,128)}, u32[]{:S(2)}) copy-start(f32[64,256]{0,1:T(8,128)} %copy.131) | copy-start | bytes 196612
  103.7 8.2 %copy-start.12 = (f32[512,32]{0,1:T(8,128)S(1)}, f32[512,32]{0,1:T(8,128)}, u32[]{:S(2)}) copy-start(f32[512,32]{0,1:T(8,128)} %param.12) | copy-start | bytes 196612
  103.7 8.2 %copy-start.13 = (f32[1,512]{1,0:T(1,128)S(1)}, f32[1,512]{1,0:T(1,128)}, u32[]{:S(2)}) copy-start(f32[1,512]{1,0:T(1,128)} %param.11) | copy-start | bytes 6148
  103.7 8.2 %copy-start.14 = (f32[32]{0:T(128)S(1)}, f32[32]{0:T(128)}, u32[]{:S(2)}) copy-start(f32[32]{0:T(128)} %param.13) | copy-start | bytes 388
  103.9 8.3 %copy-start.15 = (s32[1,4]{1,0:T(1,128)S(1)}, s32[1,4]{1,0:T(1,128)}, u32[]{:S(2)}) copy-start(s32[1,4]{1,0:T(1,128)} %param.10) | copy-start | bytes 52
  105.4 16.0 %all-to-all-start.1 = ((f32[8,1,18432]{2,1,0:T(1,128)}), f32[8,1,18432]{2,1,0:T(1,128)S(1)}, u32[]{:S(2)}, u32[]{:S(2)}) async-start(f32[8,1,18432]{2,1,0:T(1,128)} %reshape.180), calls=%async_computation.1 | async-start | bytes 1179648 | tf_op jit(solution)/shard_map/all_to_all | solution.py:40
  137.4 9.7 %all-to-all-start.2 = ((f32[8,1,64]{2,1,0:T(1,128)}), f32[8,1,64]{2,1,0:T(1,128)S(1)}, u32[]{:S(2)}, u32[]{:S(2)}) async-start(f32[8,1,64]{2,1,0:T(1,128)} %broadcast_in_dim.7), calls=%async_computation.2 | async-start | bytes 8192 | tf_op jit(solution)/shard_map/all_to_all | solution.py:24
  140.7 85.0 %all-gather.4.cloned.1.call-start = ((), (), s32[]{:S(2)}) async-start(), calls=%async_computation.4 | async-start | bytes 1474560 | tf_op jit(solution)/shard_map/all_gather | solution.py:91
  187.0 33.1 %all-to-all-start.3 = ((f32[4,1,90144]{2,1,0:T(1,128)}), f32[4,1,90144]{2,1,0:T(1,128)}, u32[]{:S(2)}, u32[]{:S(2)}) async-start(f32[4,1,90144]{2,1,0:T(1,128)} %broadcast_in_dim.8), calls=%async_computation.3 | async-start | bytes 2887680 | tf_op jit(solution)/shard_map/all_to_all | solution.py:24
  224.8 3.3 %copy-start.8 = (bf16[256,8,512]{0,2,1:T(8,128)(2,1)S(1)}, bf16[256,8,512]{0,2,1:T(8,128)(2,1)}, u32[]{:S(2)}) copy-start(bf16[256,8,512]{0,2,1:T(8,128)(2,1)} %get-tuple-element.37) | copy-start | bytes 6291460
  228.2 1.8 copy-start.7
  230.0 1.8 copy-start.6
  231.9 1.8 copy-start.5
  233.7 1.8 copy-start.4
  235.6 1.8 copy-start.3
  237.4 1.8 copy-start.2
  239.3 1.9 copy-start.9
  241.1 2.7 %copy-start.1 = (f32[4,9,64,32]{2,3,1,0:T(8,128)S(1)}, f32[4,9,64,32]{2,3,1,0:T(8,128)}, u32[]{:S(2)}) copy-start(f32[4,9,64,32]{2,3,1,0:T(8,128)} %param.9) | copy-start | bytes 884740
Sparse Core Ops, SparseCore 0:
  21.0 39.0 all-gather.7
  61.7 35.2 all-gather.5
  185.2 27.9 all-gather.3
where the time goes:
time: 251 us; the launch traced here: 250 us
  waiting for transfers between devices  64.9 us (26%)
  local copies, waits for them, and re-layouts  52.5 us (21%)
  blocking collectives  47.9 us (19%)
  matrix products  33.9 us (14%)
  starting transfers between devices  31.2 us (12%)
  between operations  14.3 us (6%)
  other arithmetic  5.74 us (2%)
    all_gather x1, waiting for transfers between devices, on_device(): lax.all_gather(feat_rim, 'chan', axis=0, tiled=True)  38.5 us
    all_gather x1, blocking collectives, on_device(): mod_rows = lax.all_gather(modulated, 'rows', axis=2, tiled=True)  29.2 us
    slice x2, local copies, waits for them, and re-layouts, tap_slice(): padded[:, first_row:first_row + height, first_col:first_col + width]  22.2 us
    all_to_all x2, starting transfers between devices, copy_for_each(): return lax.all_to_all(copies, axis, split_axis=0, concat_axis=0, tiled=True)  18.6 us
    dot_general x9, matrix products, on_device(): lax.dot_general(mine[tap_index], cotan_tap, (((0,), (0,)), ((), ())), pre...  17 us
    dot_general x9, matrix products, on_device(): lax.dot_general(cotan_flat, feat_tap, (((1,), (1,)), ((), ())), preferred...  15.4 us
    all_to_all x2, waiting for transfers between devices, copy_for_each(): return lax.all_to_all(copies, axis, split_axis=0, concat_axis=0, tiled=True)  13 us
    all_to_all x1, blocking collectives, copy_for_each(): return lax.all_to_all(copies, axis, split_axis=0, concat_axis=0, tiled=True)  12.1 us
  transfers between devices with their start and end apart: 8, of which 6 were waited for; matrix products, arithmetic and copies ran while one was open for 28% of the time, Pallas kernels for 0%

commit v1 on v0

v1 whole, which is shorter than its diff:
```python
import jax
import jax.numpy as jnp
from jax import lax
from jax.experimental import pallas as pl
from jax.experimental.pallas import tpu as pltpu
from jax.sharding import PartitionSpec as P

EPS = 1e-08
MESH = pl.DeviceIdType.MESH
ROWS, SAMPLES, CHANS = 8, 4, 4
F32, BF16 = jnp.float32, jnp.bfloat16


def lane_iota(shape):
    return lax.broadcasted_iota(jnp.int32, shape, len(shape) - 1)


def moved_right(x):
    return jnp.where(lane_iota(x.shape) == 0, 0.0, pltpu.roll(x, 1, axis=1))


def moved_left(x):
    width = x.shape[1]
    return jnp.where(lane_iota(x.shape) == width - 1, 0.0, pltpu.roll(x, width - 1, axis=1))


def over_taps(x):
    flat = jnp.sum(x, axis=(0, 1))[None, :]
    half = flat[:, :128] + flat[:, 128:]
    return half + pltpu.roll(half, 64, axis=1)


def kernel(
    x_ref, f_ref, bank_ref, sel_ref, lat_ref, aw_ref, ab_ref,
    d_ref, bg_ref, awg_ref, abg_ref,
    xbuf, fs, mm, mown, gs, gbuf, latb, selb, en, sl, kg, st, ker_ref, plain_ref,
    ag_s, ag_r, ha_s, ha_r, own_s, in_s, in_r, en_s, en_r, m_s, m_r, g_s, g_r, sl_s, sl_r, kg_s, kg_r, st_s, st_r,
):
    r, b, c = lax.axis_index("rows"), lax.axis_index("samples"), lax.axis_index("chan")
    height, ch, width = x_ref.shape
    nb, ib = bank_ref.shape[0], bank_ref.shape[2]
    left, right, opp = lax.rem(c + 3, CHANS), lax.rem(c + 1, CHANS), lax.rem(c + 2, CHANS)

    def remote(src, dst, send, recv, **where):
        return pltpu.make_async_remote_copy(
            src_ref=src, dst_ref=dst, send_sem=send, recv_sem=recv, device_id=where, device_id_type=MESH
        )

    sent = []

    def go(copy):
        copy.start()
        sent.append(copy)

    barrier = pltpu.get_barrier_semaphore()
    greeted = 0
    for dr in range(ROWS):
        for dc in range(CHANS):
            if dr or dc:
                pl.semaphore_signal(
                    barrier, inc=1,
                    device_id={"rows": lax.rem(r + dr, ROWS), "chan": lax.rem(c + dc, CHANS)},
                    device_id_type=MESH,
                )
                greeted += 1
    for db in range(1, SAMPLES):
        for dc in range(CHANS):
            pl.semaphore_signal(
                barrier, inc=1,
                device_id={"samples": lax.rem(b + db, SAMPLES), "chan": lax.rem(c + dc, CHANS)},
                device_id_type=MESH,
            )
            greeted += 1

    lat = lat_ref[...]
    latb[pl.ds(b, 1)] = jnp.broadcast_to(lat[None], (1, 8, lat.shape[1]))
    sel = sel_ref[...].astype(F32)
    selrow = jnp.zeros((8, 128), F32)
    for k in range(nb):
        selrow = jnp.where(lane_iota((8, 128)) == k, sel[:, k : k + 1], selrow)
    selb[pl.ds(b, 1)] = selrow[None]
    square = lax.broadcasted_iota(jnp.int32, (ib, ib), 0) == lane_iota((ib, ib))
    bias = jnp.sum(jnp.where(square, ab_ref[...], 0.0), axis=1, keepdims=True)
    style = jnp.sum(aw_ref[...] * lat, axis=1, keepdims=True) + bias
    ker_ref[...] = jnp.zeros_like(ker_ref)
    for kh in range(3):
        for kw in range(3):
            tap = sum(sel[:, k : k + 1] * bank_ref[k, 3 * kh + kw] for k in range(nb))
            ker_ref[kw, :, (2 - kh) * ch : (3 - kh) * ch] = tap
    ker = ker_ref[...]
    plain_ref[...] = ker * style[None]
    plain = plain_ref[...]
    en[pl.ds(r, 1)] = jnp.broadcast_to(over_taps(plain * plain)[None], (1, 8, 128))

    own = pltpu.make_async_copy(x_ref, xbuf.at[pl.ds(1, height), c], own_s)
    own.start()
    xbuf[height + 2] = jnp.zeros(xbuf.shape[1:], BF16)

    @pl.when(r == 0)
    def _():
        xbuf[0] = jnp.zeros(xbuf.shape[1:], BF16)

    @pl.when(r == ROWS - 1)
    def _():
        xbuf[height + 1] = jnp.zeros(xbuf.shape[1:], BF16)

    pl.semaphore_wait(barrier, greeted)

    for d in range(1, ROWS):
        go(remote(en.at[r], en.at[r], en_s.at[d], en_r.at[d], rows=lax.rem(r + d, ROWS)))
    half = height // 2
    quarter = height // 4

    def rows_of(shard, first, count):
        return xbuf.at[pl.ds(first + 1, count), shard]

    to_right, to_left = {"chan": right}, {"chan": left}
    go(remote(x_ref.at[pl.ds(0, half)], rows_of(c, 0, half), ag_s.at[0, 0], ag_r.at[0, 0], **to_right))
    go(remote(x_ref.at[pl.ds(half, half)], rows_of(c, half, half), ag_s.at[1, 0], ag_r.at[1, 0], **to_left))

    def halo(i, shard, top, from_own):
        at = 0 if top else height - 1
        src = x_ref.at[pl.ds(at, 1)] if from_own else rows_of(shard, at, 1)
        dst = xbuf.at[pl.ds(height + 1 if top else 0, 1), shard]
        there = jnp.maximum(r - 1, 0) if top else jnp.minimum(r + 1, ROWS - 1)
        side = 0 if top else 1
        return remote(src, dst, ha_s.at[i, side], ha_r.at[i, side], rows=there)

    def start_halo(i, shard, top, from_own=False):
        @pl.when(r > 0 if top else r < ROWS - 1)
        def _():
            halo(i, shard, top, from_own).start()

    def wait_halo(i, shard):
        @pl.when(r < ROWS - 1)
        def _():
            halo(i, shard, True, False).wait_recv()

        @pl.when(r > 0)
        def _():
            halo(i, shard, False, False).wait_recv()

    start_halo(0, c, True, True)
    start_halo(0, c, False, True)
    go(remote(x_ref.at[pl.ds(half, half)], rows_of(c, half, half), ag_s.at[0, 1], ag_r.at[0, 1], **to_right))
    go(remote(x_ref.at[pl.ds(0, half)], rows_of(c, 0, half), ag_s.at[1, 1], ag_r.at[1, 1], **to_left))
    for d in range(1, SAMPLES):
        there = lax.rem(b + d, SAMPLES)
        go(remote(latb.at[b], latb.at[b], in_s.at[0, d], in_r.at[0, d], samples=there))
        go(remote(selb.at[b], selb.at[b], in_s.at[1, d], in_r.at[1, d], samples=there))

    def shifted(h, carry):
        f = f_ref[h]
        wide = f.astype(F32)
        fs[h, 0:ch] = moved_right(wide).astype(BF16)
        fs[h, ch : 2 * ch] = f
        fs[h, 2 * ch : 3 * ch] = moved_left(wide).astype(BF16)
        return carry

    lax.fori_loop(0, height, shifted, 0)

    for d in range(1, ROWS):
        src = lax.rem(r + ROWS - d, ROWS)
        remote(en.at[src], en.at[src], en_s.at[d], en_r.at[d], rows=src).wait_recv()
    scale = lax.rsqrt(jnp.sum(en[...], axis=0)[0:1] + EPS)
    scale = jnp.concatenate([scale, scale], axis=1)[None]
    mown[...] = (plain * scale).astype(BF16)
    home = r // 2
    place = pl.multiple_of(lax.rem(r, 2) * ib, ib)

    def mm_block(row, chan):
        return mm.at[chan, :, pl.ds(pl.multiple_of(lax.rem(row, 2) * ib, ib), ib), :]

    mine = mm_block(r, c)
    for d in range(1, ROWS):
        go(remote(mown, mine, m_s.at[d], m_r.at[lax.rem(r, 2), c], rows=lax.rem(r + d, ROWS), chan=home))
    m_here = remote(mown, mine, m_s.at[0], m_r.at[lax.rem(r, 2), c], chan=home)
    m_local = pltpu.make_async_copy(mown, mine, m_r.at[lax.rem(r, 2), c])

    @pl.when(home == c)
    def _():
        m_local.start()

    @pl.when(home != c)
    def _():
        m_here.start()

    def grad_of(i, shard):
        def step(h, acc):
            around = xbuf[pl.ds(h, 4), shard].reshape(4 * ch, width)
            return acc + lax.dot_general(
                fs[h], around, (((1,), (1,)), ((), ())), preferred_element_type=F32
            )

        acc = lax.fori_loop(0, height, step, jnp.zeros((3 * ch, 4 * ch), F32))
        gs[i] = acc.reshape(3, ch, 4 * ch).astype(BF16)
        for part in range(2):
            src = gs.at[i, :, pl.ds(part * ib, ib), :]
            target = 2 * c + part
            if i == 0:
                @pl.when(target == r)
                def _():
                    pltpu.make_async_copy(src, gbuf.at[r], g_r.at[r]).start()

                @pl.when(target != r)
                def _():
                    remote(src, gbuf.at[r], g_s.at[i, part], g_r.at[r], rows=target).start()
            else:
                go(remote(src, gbuf.at[r], g_s.at[i, part], g_r.at[r], rows=target, chan=shard))

    own.wait()
    wait_halo(0, c)
    grad_of(0, c)

    def from_left(k, first, count, shard):
        return remote(rows_of(shard, first, count), rows_of(shard, first, count), ag_s.at[0, k], ag_r.at[0, k], **to_right)

    def from_right(k, first, count, shard):
        return remote(rows_of(shard, first, count), rows_of(shard, first, count), ag_s.at[1, k], ag_r.at[1, k], **to_left)

    from_left(0, 0, half, left).wait_recv()
    go(from_left(2, 0, quarter, left))
    go(from_left(3, quarter, quarter, left))
    start_halo(1, left, True)
    from_right(0, half, half, right).wait_recv()
    go(from_right(2, height - quarter, quarter, right))
    go(from_right(3, half, quarter, right))
    start_halo(2, right, False)
    from_left(1, half, half, left).wait_recv()
    start_halo(1, left, False)
    from_right(1, 0, half, right).wait_recv()
    start_halo(2, right, True)
    wait_halo(1, left)
    grad_of(1, left)
    wait_halo(2, right)
    grad_of(2, right)
    from_left(2, 0, quarter, opp).wait_recv()
    start_halo(3, opp, True)
    from_right(2, height - quarter, quarter, opp).wait_recv()
    start_halo(3, opp, False)
    from_left(3, quarter, quarter, opp).wait_recv()
    from_right(3, half, quarter, opp).wait_recv()
    wait_halo(3, opp)
    grad_of(3, opp)

    for part in range(2):
        for chan in range(CHANS):
            remote(mown, mm_block(part, chan), m_s.at[0], m_r.at[part, chan], chan=home).wait_recv()

    def rows_out(h, carry):
        total = jnp.zeros((3 * ch, width), F32)
        for shard in range(CHANS):
            around = xbuf[pl.ds(h, 4), shard].reshape(4 * ch, width)
            total = total + jnp.dot(mm[shard].reshape(3 * ch, 4 * ch), around, preferred_element_type=F32)
        out = total[ch : 2 * ch] + moved_left(total[:ch]) + moved_right(total[2 * ch :])
        d_ref[h] = out.astype(BF16)
        return carry

    lax.fori_loop(0, height, rows_out, 0)

    for src in range(ROWS):
        remote(gs.at[0, :, pl.ds(0, ib), :], gbuf.at[src], g_s.at[0, 0], g_r.at[src], rows=home).wait_recv()
    grad = gbuf[0].astype(F32)
    for src in range(1, ROWS):
        grad = grad + gbuf[src].astype(F32)
    sl[pl.ds(r, 1)] = jnp.broadcast_to(over_taps(grad * plain)[None], (1, 8, 128))
    for d in range(1, ROWS):
        go(remote(sl.at[r], sl.at[r], sl_s.at[d], sl_r.at[d], rows=lax.rem(r + d, ROWS)))
    for d in range(1, ROWS):
        src = lax.rem(r + ROWS - d, ROWS)
        remote(sl.at[src], sl.at[src], sl_s.at[d], sl_r.at[d], rows=src).wait_recv()
    slope = jnp.sum(sl[...], axis=0)[0:1]
    slope = jnp.concatenate([slope, slope], axis=1)[None]
    plain_grad = grad * scale - plain * (slope * (scale * scale * scale))
    kg[pl.ds(b, 1)] = (plain_grad * style[None])[None]
    for d in range(1, SAMPLES):
        go(remote(kg.at[b], kg.at[b], kg_s.at[d], kg_r.at[d], samples=lax.rem(b + d, SAMPLES)))
    by_input = jnp.sum(plain_grad * ker, axis=0)
    by_input = jnp.concatenate([by_input, jnp.zeros((128 - ib, by_input.shape[1]), F32)], axis=0)
    style_part = lax.dot_general(
        jnp.ones((8, by_input.shape[1]), F32), by_input, (((1,), (1,)), ((), ())),
        preferred_element_type=F32, precision=lax.Precision.HIGHEST,
    )
    st[pl.ds(b, 1), pl.ds(c, 1)] = style_part[None, None]
    for db in range(SAMPLES):
        for dc in range(CHANS):
            if db or dc:
                go(remote(
                    st.at[b, c], st.at[b, c], st_s.at[db, dc], st_r.at[db, dc],
                    samples=lax.rem(b + db, SAMPLES), chan=lax.rem(c + dc, CHANS),
                ))

    for d in range(1, SAMPLES):
        src = lax.rem(b + SAMPLES - d, SAMPLES)
        remote(latb.at[src], latb.at[src], in_s.at[0, d], in_r.at[0, d], samples=src).wait_recv()
        remote(selb.at[src], selb.at[src], in_s.at[1, d], in_r.at[1, d], samples=src).wait_recv()
    for db in range(SAMPLES):
        for dc in range(CHANS):
            if db or dc:
                bs, cs = lax.rem(b + SAMPLES - db, SAMPLES), lax.rem(c + CHANS - dc, CHANS)
                remote(
                    st.at[bs, cs], st.at[bs, cs], st_s.at[db, dc], st_r.at[db, dc], samples=bs, chan=cs
                ).wait_recv()
    diagonal = lax.broadcasted_iota(jnp.int32, (ib, 128), 0) == lane_iota((ib, 128))
    style_sum = jnp.zeros((1, 128), F32)
    affine = jnp.zeros(awg_ref.shape, F32)
    for s in range(SAMPLES):
        row = st[s, 0] + st[s, 1] + st[s, 2] + st[s, 3]
        row = row[0:1]
        style_sum = style_sum + row
        column = jnp.sum(jnp.where(diagonal, row, 0.0), axis=1, keepdims=True)
        affine = affine + column * latb[s][0:1]
    awg_ref[...] = affine
    abg_ref[...] = style_sum[:, :ib]
    for d in range(1, SAMPLES):
        src = lax.rem(b + SAMPLES - d, SAMPLES)
        remote(kg.at[src], kg.at[src], kg_s.at[d], kg_r.at[d], samples=src).wait_recv()
    for k in range(nb):
        weights = [selb[s][0:1, k : k + 1] for s in range(SAMPLES)]
        for kw in range(3):
            total = sum(weights[s] * kg[s, kw] for s in range(SAMPLES))
            for kh in range(3):
                bg_ref[k, 3 * kh + kw] = total[:, (2 - kh) * ch : (3 - kh) * ch]

    for copy in sent:
        copy.wait_send()

    @pl.when(home != c)
    def _():
        m_here.wait_send()

    for part in range(2):
        @pl.when(2 * c + part != r)
        def _():
            remote(
                gs.at[0, :, pl.ds(part * ib, ib), :], gbuf.at[r], g_s.at[0, part], g_r.at[r], rows=2 * c + part
            ).wait_send()

    for i, shard in enumerate((c, left, right, opp)):
        @pl.when(r > 0)
        def _():
            halo(i, shard, True, False).wait_send()

        @pl.when(r < ROWS - 1)
        def _():
            halo(i, shard, False, False).wait_send()


def on_device(feature, out_grad, bank, select, latent, affine_w, affine_b):
    x = jnp.transpose(out_grad[0], (1, 0, 2))
    f = jnp.transpose(feature[0], (1, 0, 2))
    height, ch, width = x.shape
    nb, taps, _, ib = bank.shape
    z = latent.shape[1]
    lanes = 4 * ch
    vmem = pl.BlockSpec(memory_space=pltpu.VMEM)
    dma = pltpu.SemaphoreType.DMA
    d, bg, awg, abg = pl.pallas_call(
        kernel,
        out_shape=(
            jax.ShapeDtypeStruct((height, ch, width), BF16),
            jax.ShapeDtypeStruct((nb, taps, ib, ch), F32),
            jax.ShapeDtypeStruct((ib, z), F32),
            jax.ShapeDtypeStruct((1, ib), F32),
        ),
        in_specs=[vmem] * 7,
        out_specs=(vmem,) * 4,
        scratch_shapes=[
            pltpu.VMEM((height + 3, CHANS, ch, width), BF16),
            pltpu.VMEM((height, 3 * ch, width), BF16),
            pltpu.VMEM((CHANS, 3, ch, lanes), BF16),
            pltpu.VMEM((3, ib, lanes), BF16),
            pltpu.VMEM((CHANS, 3, ch, lanes), BF16),
            pltpu.VMEM((ROWS, 3, ib, lanes), BF16),
            pltpu.VMEM((SAMPLES, 8, z), F32),
            pltpu.VMEM((SAMPLES, 8, 128), F32),
            pltpu.VMEM((ROWS, 8, 128), F32),
            pltpu.VMEM((ROWS, 8, 128), F32),
            pltpu.VMEM((SAMPLES, 3, ib, lanes), F32),
            pltpu.VMEM((SAMPLES, CHANS, 8, 128), F32),
            pltpu.VMEM((3, ib, lanes), F32),
            pltpu.VMEM((3, ib, lanes), F32),
            dma((2, 4)), dma((2, 4)),
            dma((4, 2)), dma((4, 2)),
            dma,
            dma((2, SAMPLES)), dma((2, SAMPLES)),
            dma((ROWS,)), dma((ROWS,)),
            dma((ROWS,)), dma((2, CHANS)),
            dma((CHANS, 2)), dma((ROWS,)),
            dma((ROWS,)), dma((ROWS,)),
            dma((SAMPLES,)), dma((SAMPLES,)),
            dma((SAMPLES, CHANS)), dma((SAMPLES, CHANS)),
        ],
        compiler_params=pltpu.CompilerParams(
            collective_id=0, has_side_effects=True, vmem_limit_bytes=48 * 1024 * 1024
        ),
    )(
        x, f, jnp.transpose(bank, (0, 1, 3, 2)), select, latent,
        jnp.transpose(affine_w), affine_b[None],
    )
    return (
        jnp.transpose(d, (1, 0, 2))[None],
        jnp.transpose(bg, (0, 1, 3, 2)),
        jnp.transpose(awg),
        abg[0],
    )


def solution(mesh):
    return jax.shard_map(
        on_device,
        mesh=mesh,
        in_specs=(
            P("samples", "chan", "rows", None),
            P("samples", "chan", "rows", None),
            P(None, None, "chan", "rows"),
            P("samples", None),
            P("samples", None),
            P(None, "rows"),
            P("rows"),
        ),
        out_specs=(
            P("samples", "chan", "rows", None),
            P(None, None, "chan", "rows"),
            P(None, "rows"),
            P("rows"),
        ),
        check_vma=False,
    )
```

time: 251 us -> 70.9 us (0.28)
  waiting for transfers between devices: 64.9 us -> 0 us
  Pallas kernels: 0 us -> 64.7 us
  blocking collectives: 47.9 us -> 0 us
  local copies, waits for them, and re-layouts: 52.5 us -> 5.27 us
  matrix products: 33.9 us -> 0 us
  starting transfers between devices: 31.2 us -> 0 us
  between operations: 14.3 us -> 0.7 us
  other arithmetic: 5.74 us -> 0 us
    pallas_call x0 -> x1, Pallas kernels: none -> 64.7 us  [on_device(): pl.pallas_call(kernel, out_shape=(jax.ShapeDtypeStruct((height, ch, width...]
    all_gather x3 -> x0, waiting for transfers between devices: 38.5 us -> none  [the longest x1 38.5 us: on_device(): lax.all_gather(feat_rim, 'chan', axis=0, tiled=True)]
    dot_general x20 -> x0, matrix products: 33.9 us -> none  [the longest x9 17 us: on_device(): lax.dot_general(mine[tap_index], cotan_tap, (((0,), (0,)), ((), ())), pre...]
    all_gather x1 -> x0, blocking collectives: 29.2 us -> none  [on_device(): mod_rows = lax.all_gather(modulated, 'rows', axis=2, tiled=True)]
    all_to_all x3 -> x0, starting transfers between devices: 25.2 us -> none  [the longest x2 18.6 us: copy_for_each(): return lax.all_to_all(copies, axis, split_axis=0, concat_axis=0, tiled=True)]
    slice x6 -> x0, local copies, waits for them, and re-layouts: 23.9 us -> none  [the longest x2 22.2 us: tap_slice(): padded[:, first_row:first_row + height, first_col:first_col + width]]
    all_to_all x3 -> x0, waiting for transfers between devices: 20.8 us -> none  [the longest x2 13 us: copy_for_each(): return lax.all_to_all(copies, axis, split_axis=0, concat_axis=0, tiled=True)]
    all_to_all x1 -> x0, blocking collectives: 12.1 us -> none  [copy_for_each(): return lax.all_to_all(copies, axis, split_axis=0, concat_axis=0, tiled=True)]
  transfers between devices with their start and end apart: 8 -> 0, of which waited for: 6 -> 0; matrix products, arithmetic and copies ran while one was open for 28% -> 0% of each run, Pallas kernels for 0% -> 0%
where the time goes in v1:
time: 70.9 us; the launch traced here: 70.7 us
  Pallas kernels  64.7 us (91%)
  local copies, waits for them, and re-layouts  5.27 us (7%)
    pallas_call x1, Pallas kernels, on_device(): pl.pallas_call(kernel, out_shape=(jax.ShapeDtypeStruct((height, ch, width...  64.7 us
    unnamed x14, local copies, waits for them, and re-layouts  3.69 us
    transpose x1, local copies, waits for them, and re-layouts, on_device(): f = jnp.transpose(feature[0], (1, 0, 2))  1.58 us

profile of v1, /device:TPU:1, one launch (start us, length us, event | category | flops | bytes accessed | tf_op | source)
XLA Modules:
  0.0 70.7 jit_solution(909592256677083466)
XLA Ops:
  0.6 0.0 copy-start
  0.6 0.0 copy-start.1
  0.7 1.6 %copy_bitcast_fusion = (bf16[8,64,512]{2,1,0:T(8,128)(2,1)S(1)}, bf16[8,64,512]{2,1,0:T(8,128)(2,1)S(1)}) fusion(bf16[1,64,8,512]{3,2,1,0:T(8,128)(2,1)} %param.7, bf16[1,64,8,512]{3,2,1,0:T(8,128)(2,1)} %param.8), kind=kLoop, calls=%fused_computation | loop fusion | bytes 2097152 | tf_op jit(solution)/shard_map/transpose | solution.py:351
  2.2 0.0 copy-start.2
  2.2 0.0 copy-start.3
  2.3 0.0 copy-start.4
  2.3 0.0 copy-done
  2.3 0.0 copy-done.1
  2.3 0.6 copy-done.2
  2.9 0.0 copy-done.3
  2.9 0.0 copy-done.4
  2.9 64.7 %shard_map.102 = (bf16[8,64,512]{2,1,0:T(8,128)(2,1)S(1)}, f32[4,9,32,64]{3,2,1,0:T(8,128)S(1)}, f32[32,512]{1,0:T(8,128)S(1)}, f32[1,32]{1,0:T(1,128)S(1)}) custom-call(bf16[8,64,512]{2,1,0:T(8,128)(2,1)S(1)} %get-tuple-element.17.x_ref, bf16[8,64,512]{2,1,0:T(8,128)(2,1)S(1)} %get-tuple-element.16.f_ref, f32[4,9,32,64]{3,2,1,0:T(8,128)S(1)} %bitcast.17, ...), custom_call_target="tpu_custom_call" | custom-call | tf_op jit(solution)/shard_map/pallas_call | solution.py:358
  67.7 1.1 %copy.13 = bf16[1,64,8,512]{3,2,1,0:T(8,128)(2,1)} copy(bf16[1,64,8,512]{3,1,2,0:T(8,128)(2,1)S(1)} %bitcast.19) | data formatting | bytes 1048576
  68.8 0.8 %copy.19 = f32[4,9,64,32]{2,3,1,0:T(8,128)} copy(f32[4,9,64,32]{2,3,1,0:T(8,128)S(1)} %bitcast.18) | data formatting | bytes 589824
  69.6 0.6 copy.20
  70.2 0.5 copy.21
Async XLA Ops:
  0.6 1.6 %copy-start = (f32[4,9,64,32]{2,3,1,0:T(8,128)S(1)}, f32[4,9,64,32]{2,3,1,0:T(8,128)}, u32[]{:S(2)}) copy-start(f32[4,9,64,32]{2,3,1,0:T(8,128)} %param.9) | copy-start | bytes 884740
  0.6 1.6 %copy-start.1 = (f32[512,32]{0,1:T(8,128)S(1)}, f32[512,32]{0,1:T(8,128)}, u32[]{:S(2)}) copy-start(f32[512,32]{0,1:T(8,128)} %param.12) | copy-start | bytes 196612
  2.2 0.7 copy-start.2
  2.2 0.7 copy-start.3
  2.3 0.7 copy-start.4

commit v2 on v1

v2 whole, which is shorter than its diff:
```python
import jax
import jax.numpy as jnp
from jax import lax
from jax.experimental import pallas as pl
from jax.experimental.pallas import tpu as pltpu
from jax.sharding import PartitionSpec as P

EPS = 1e-08
MESH = pl.DeviceIdType.MESH
ROWS, SAMPLES, CHANS = 8, 4, 4
F32, BF16 = jnp.float32, jnp.bfloat16


def lane_iota(shape):
    return lax.broadcasted_iota(jnp.int32, shape, len(shape) - 1)


def moved_right(x):
    return jnp.where(lane_iota(x.shape) == 0, 0.0, pltpu.roll(x, 1, axis=1))


def moved_left(x):
    width = x.shape[1]
    return jnp.where(lane_iota(x.shape) == width - 1, 0.0, pltpu.roll(x, width - 1, axis=1))


def over_taps(x):
    flat = jnp.sum(x, axis=(0, 1))[None, :]
    half = flat[:, :128] + flat[:, 128:]
    return half + pltpu.roll(half, 64, axis=1)


def kernel(
    x_ref, f_ref, bank_ref, sel_ref, lat_ref, aw_ref, ab_ref,
    d_ref, bg_ref, awg_ref, abg_ref,
    xbuf, fs, fhalo, mr, mm, gs, gbuf, latb, selb, en, slv, slo, kg, st, ker_ref, plain_ref, dacc, dsend, dhalo,
    ag_s, ag_r, fh_s, fh_r, dh_s, dh_r, own_s, in_s, in_r, en_s, en_r, mz_s, mf_s, my_s, mr_r, my_r,
    g_s, g_r, sl_s, sl_r, kg_s, kg_r, st_s, st_r,
):
    r, b, c = lax.axis_index("rows"), lax.axis_index("samples"), lax.axis_index("chan")
    height, ch, width = x_ref.shape
    nb, ib = bank_ref.shape[0], bank_ref.shape[2]
    left, right, opp = lax.rem(c + 3, CHANS), lax.rem(c + 1, CHANS), lax.rem(c + 2, CHANS)
    tall = 6 * ib

    def remote(src, dst, send, recv, **where):
        return pltpu.make_async_remote_copy(
            src_ref=src, dst_ref=dst, send_sem=send, recv_sem=recv, device_id=where, device_id_type=MESH
        )

    sent = []

    def go(copy):
        copy.start()
        sent.append(copy)

    barrier = pltpu.get_barrier_semaphore()
    greeted = 0
    for dr in range(ROWS):
        for dc in range(CHANS):
            if dr or dc:
                pl.semaphore_signal(
                    barrier, inc=1,
                    device_id={"rows": lax.rem(r + dr, ROWS), "chan": lax.rem(c + dc, CHANS)},
                    device_id_type=MESH,
                )
                greeted += 1
    for db in range(1, SAMPLES):
        for dc in range(CHANS):
            pl.semaphore_signal(
                barrier, inc=1,
                device_id={"samples": lax.rem(b + db, SAMPLES), "chan": lax.rem(c + dc, CHANS)},
                device_id_type=MESH,
            )
            greeted += 1

    lat = lat_ref[...]
    latb[pl.ds(b, 1)] = jnp.broadcast_to(lat[None], (1, 8, lat.shape[1]))
    sel = sel_ref[...].astype(F32)
    selrow = jnp.zeros((8, 128), F32)
    for k in range(nb):
        selrow = jnp.where(lane_iota((8, 128)) == k, sel[:, k : k + 1], selrow)
    selb[pl.ds(b, 1)] = selrow[None]
    square = lax.broadcasted_iota(jnp.int32, (ib, ib), 0) == lane_iota((ib, ib))
    bias = jnp.sum(jnp.where(square, ab_ref[...], 0.0), axis=1, keepdims=True)
    style = jnp.sum(aw_ref[...] * lat, axis=1, keepdims=True) + bias
    ker_ref[...] = jnp.zeros_like(ker_ref)
    for kh in range(3):
        for kw in range(3):
            tap = sum(sel[:, k : k + 1] * bank_ref[k, 3 * kh + kw] for k in range(nb))
            ker_ref[kw, :, (2 - kh) * ch : (3 - kh) * ch] = tap
    ker = ker_ref[...]
    plain_ref[...] = ker * style[None]
    plain = plain_ref[...]
    en[pl.ds(r, 1)] = over_taps(plain * plain)[None]

    own = pltpu.make_async_copy(x_ref, xbuf.at[pl.ds(2, height), c], own_s)
    own.start()

    def shift_into(at, f):
        wide = f.astype(F32)
        for kw, moved in enumerate((moved_right(wide).astype(BF16), f, moved_left(wide).astype(BF16))):
            for part in range(2):
                first = (3 * part + kw) * ib
                fs[at, first : first + ib] = moved[part * ib : (part + 1) * ib]

    def shifted(h, carry):
        shift_into(h + 1, f_ref[h])
        return carry

    lax.fori_loop(0, height, shifted, 0)
    for row in (0, 1, height + 2, height + 3, height + 4):
        xbuf[row] = jnp.zeros(xbuf.shape[1:], BF16)

    pl.semaphore_wait(barrier, greeted)

    for d in range(1, ROWS):
        go(remote(en.at[r], en.at[r], en_s.at[d], en_r.at[d], rows=lax.rem(r + d, ROWS)))
    half = height // 2
    quarter = height // 4

    def rows_of(shard, first, count):
        return xbuf.at[pl.ds(first + 2, count), shard]

    to_right, to_left = {"chan": right}, {"chan": left}
    go(remote(x_ref.at[pl.ds(0, half)], rows_of(c, 0, half), ag_s.at[0, 0], ag_r.at[0, 0], **to_right))
    go(remote(x_ref.at[pl.ds(half, half)], rows_of(c, half, half), ag_s.at[1, 0], ag_r.at[1, 0], **to_left))

    def edge(src, dst, send, recv, up):
        there = jnp.maximum(r - 1, 0) if up else jnp.minimum(r + 1, ROWS - 1)
        i = 0 if up else 1
        return remote(src, dst.at[1 - i], send.at[i], recv.at[1 - i], rows=there)

    not_first, not_last = r > 0, r < ROWS - 1

    @pl.when(not_first)
    def _():
        edge(f_ref.at[0], fhalo, fh_s, fh_r, True).start()

    @pl.when(not_last)
    def _():
        edge(f_ref.at[height - 1], fhalo, fh_s, fh_r, False).start()

    go(remote(x_ref.at[pl.ds(half, half)], rows_of(c, half, half), ag_s.at[0, 1], ag_r.at[0, 1], **to_right))
    go(remote(x_ref.at[pl.ds(0, half)], rows_of(c, 0, half), ag_s.at[1, 1], ag_r.at[1, 1], **to_left))
    for d in range(1, SAMPLES):
        there = lax.rem(b + d, SAMPLES)
        go(remote(latb.at[b], latb.at[b], in_s.at[0, d], in_r.at[0, d], samples=there))
        go(remote(selb.at[b], selb.at[b], in_s.at[1, d], in_r.at[1, d], samples=there))

    for d in range(1, ROWS):
        src = lax.rem(r + ROWS - d, ROWS)
        remote(en.at[src], en.at[src], en_s.at[d], en_r.at[d], rows=src).wait_recv()
    scale = lax.rsqrt(jnp.sum(en[...], axis=0) + EPS)
    scale = jnp.concatenate([scale, scale], axis=1)[None]

    mr[pl.ds(r, 1)] = (plain * scale).astype(BF16)[None]
    side, level = r // 4, lax.rem(r, 4)
    across = lax.rem(r + 4, ROWS)
    go(remote(mr.at[r], mr.at[r], mz_s.at[0], mr_r.at[0], rows=across))

    def peer(d):
        return 4 * side + lax.rem(level + d, 4)

    def far(d):
        return 4 * (1 - side) + lax.rem(level + d, 4)

    for d in range(1, 4):
        go(remote(mr.at[r], mr.at[r], mz_s.at[d], mr_r.at[d], rows=peer(d)))

    @pl.when(not_first)
    def _():
        edge(f_ref.at[0], fhalo, fh_s, fh_r, False).wait_recv()
        shift_into(0, fhalo[0])

    @pl.when(r == 0)
    def _():
        fs[0] = jnp.zeros(fs.shape[1:], BF16)

    @pl.when(not_last)
    def _():
        edge(f_ref.at[0], fhalo, fh_s, fh_r, True).wait_recv()
        shift_into(height + 1, fhalo[1])

    @pl.when(r == ROWS - 1)
    def _():
        fs[height + 1] = jnp.zeros(fs.shape[1:], BF16)

    def grad_of(i, shard):
        def step(q, acc):
            around = xbuf[pl.ds(q, 4), shard].reshape(4 * ch, width)
            return acc + lax.dot_general(
                fs[q], around, (((1,), (1,)), ((), ())), preferred_element_type=F32
            )

        acc = lax.fori_loop(0, height + 2, step, jnp.zeros((tall, 4 * ch), F32))
        gs[i] = acc.reshape(2, 3, ib, 4 * ch).astype(BF16)
        for part in range(2):
            src = gs.at[i, part]
            target = 2 * c + part
            if i == 0:
                @pl.when(target == r)
                def _():
                    pltpu.make_async_copy(src, gbuf.at[r], g_r.at[r]).start()

                @pl.when(target != r)
                def _():
                    remote(src, gbuf.at[r], g_s.at[i, part], g_r.at[r], rows=target).start()
            else:
                go(remote(src, gbuf.at[r], g_s.at[i, part], g_r.at[r], rows=target, chan=shard))

    own.wait()
    remote(mr.at[across], mr.at[across], mz_s.at[0], mr_r.at[0], rows=across).wait_recv()
    for d in range(1, 4):
        go(remote(mr.at[across], mr.at[across], mf_s.at[d], mr_r.at[4 + d], rows=peer(d)))

    grad_of(0, c)

    def from_left(k, first, count, shard):
        return remote(rows_of(shard, first, count), rows_of(shard, first, count), ag_s.at[0, k], ag_r.at[0, k], **to_right)

    def from_right(k, first, count, shard):
        return remote(rows_of(shard, first, count), rows_of(shard, first, count), ag_s.at[1, k], ag_r.at[1, k], **to_left)

    from_left(0, 0, half, left).wait_recv()
    go(from_left(2, 0, quarter, left))
    from_right(0, half, half, right).wait_recv()
    go(from_right(2, height - quarter, quarter, right))

    for d in range(1, 4):
        src = peer(4 - d)
        remote(mr.at[src], mr.at[src], mz_s.at[d], mr_r.at[d], rows=src).wait_recv()
        src = far(4 - d)
        remote(mr.at[src], mr.at[src], mf_s.at[d], mr_r.at[4 + d], rows=across).wait_recv()
    for d in (1, 3, 2):
        there = lax.rem(c + d, CHANS)
        go(remote(mr.at[pl.ds(2 * there, 2)], mm.at[c], my_s.at[d], my_r.at[d], chan=there))
    mine = pltpu.make_async_copy(mr.at[pl.ds(2 * c, 2)], mm.at[c], my_r.at[0])
    mine.start()
    go(from_left(3, quarter, quarter, left))
    go(from_right(3, half, quarter, right))

    from_left(1, half, half, left).wait_recv()

    grad_of(1, left)

    from_right(1, 0, half, right).wait_recv()

    grad_of(2, right)

    from_left(2, 0, quarter, opp).wait_recv()
    from_right(2, height - quarter, quarter, opp).wait_recv()

    from_left(3, quarter, quarter, opp).wait_recv()
    from_right(3, half, quarter, opp).wait_recv()

    grad_of(3, opp)

    for d in range(1, CHANS):
        src = lax.rem(c + CHANS - d, CHANS)
        remote(mr.at[pl.ds(0, 2)], mm.at[src], my_s.at[d], my_r.at[d], chan=src).wait_recv()
    mine.wait()

    for i, (k, shard) in enumerate(((0, c), (3, left), (1, right), (2, opp))):
        parts = gs[i].astype(F32) * mm[shard].astype(F32)
        slo[i] = over_taps(parts[0] + parts[1])
        for d in range(ROWS):
            if k == 0 and d == 0:
                slv[pl.ds(r, 1), pl.ds(c, 1)] = slo[0][None, None]
            else:
                go(remote(
                    slo.at[i], slv.at[r, c], sl_s.at[d, k], sl_r.at[d, k], rows=lax.rem(r + d, ROWS), chan=shard
                ))

    def rows_out(q, carry):
        total = jnp.zeros((tall, width), F32)
        for shard in range(CHANS):
            around = xbuf[pl.ds(q, 4), shard].reshape(4 * ch, width)
            total = total + jnp.dot(mm[shard].reshape(tall, 4 * ch), around, preferred_element_type=F32)
        for part in range(2):
            t = total[3 * part * ib : 3 * (part + 1) * ib]
            dacc[q, part * ib : (part + 1) * ib] = t[ib : 2 * ib] + moved_left(t[:ib]) + moved_right(t[2 * ib :])
        return carry

    lax.fori_loop(0, height + 2, rows_out, 0)
    dsend[0] = dacc[0].astype(BF16)
    dsend[1] = dacc[height + 1].astype(BF16)

    @pl.when(not_first)
    def _():
        edge(dsend.at[0], dhalo, dh_s, dh_r, True).start()

    @pl.when(not_last)
    def _():
        edge(dsend.at[1], dhalo, dh_s, dh_r, False).start()

    for src in range(ROWS):
        remote(gs.at[0, 0], gbuf.at[src], g_s.at[0, 0], g_r.at[src], rows=across).wait_recv()

    for d in range(ROWS):
        for k in range(CHANS):
            if d or k:
                rs, cs = lax.rem(r + ROWS - d, ROWS), lax.rem(c + CHANS - k, CHANS)
                remote(slo.at[0], slv.at[rs, cs], sl_s.at[d, k], sl_r.at[d, k], rows=rs, chan=cs).wait_recv()

    grad = gbuf[0].astype(F32)
    for src in range(1, ROWS):
        grad = grad + gbuf[src].astype(F32)
    slope = jnp.sum(slv[...], axis=(0, 1))
    slope = jnp.concatenate([slope, slope], axis=1)[None]
    plain_grad = grad * scale - plain * (slope * (scale * scale))
    by_input = jnp.sum(plain_grad * ker, axis=0)
    by_input = jnp.concatenate([by_input, jnp.zeros((128 - ib, by_input.shape[1]), F32)], axis=0)
    style_part = lax.dot_general(
        jnp.ones((8, by_input.shape[1]), F32), by_input, (((1,), (1,)), ((), ())),
        preferred_element_type=F32, precision=lax.Precision.HIGHEST,
    )
    st[pl.ds(b, 1), pl.ds(c, 1)] = style_part[0:1][None, None]
    for db in range(SAMPLES):
        for dc in range(CHANS):
            if db or dc:
                go(remote(
                    st.at[b, c], st.at[b, c], st_s.at[db, dc], st_r.at[db, dc],
                    samples=lax.rem(b + db, SAMPLES), chan=lax.rem(c + dc, CHANS),
                ))
    kg[pl.ds(b, 1)] = (plain_grad * style[None])[None].astype(BF16)
    for d in range(1, SAMPLES):
        go(remote(kg.at[b], kg.at[b], kg_s.at[d], kg_r.at[d], samples=lax.rem(b + d, SAMPLES)))

    for h in range(1, height - 1):
        d_ref[h] = dacc[h + 1].astype(BF16)

    @pl.when(r == 0)
    def _():
        d_ref[0] = dacc[1].astype(BF16)

    @pl.when(not_first)
    def _():
        edge(dsend.at[0], dhalo, dh_s, dh_r, False).wait_recv()
        d_ref[0] = (dacc[1] + dhalo[0].astype(F32)).astype(BF16)

    @pl.when(r == ROWS - 1)
    def _():
        d_ref[height - 1] = dacc[height].astype(BF16)

    @pl.when(not_last)
    def _():
        edge(dsend.at[0], dhalo, dh_s, dh_r, True).wait_recv()
        d_ref[height - 1] = (dacc[height] + dhalo[1].astype(F32)).astype(BF16)

    for d in range(1, SAMPLES):
        src = lax.rem(b + SAMPLES - d, SAMPLES)
        remote(latb.at[src], latb.at[src], in_s.at[0, d], in_r.at[0, d], samples=src).wait_recv()
        remote(selb.at[src], selb.at[src], in_s.at[1, d], in_r.at[1, d], samples=src).wait_recv()
    for db in range(SAMPLES):
        for dc in range(CHANS):
            if db or dc:
                bs, cs = lax.rem(b + SAMPLES - db, SAMPLES), lax.rem(c + CHANS - dc, CHANS)
                remote(
                    st.at[bs, cs], st.at[bs, cs], st_s.at[db, dc], st_r.at[db, dc], samples=bs, chan=cs
                ).wait_recv()

    diagonal = lax.broadcasted_iota(jnp.int32, (ib, 128), 0) == lane_iota((ib, 128))
    style_sum = jnp.zeros((1, 128), F32)
    affine = jnp.zeros(awg_ref.shape, F32)
    for s in range(SAMPLES):
        row = st[s, 0] + st[s, 1] + st[s, 2] + st[s, 3]
        style_sum = style_sum + row
        column = jnp.sum(jnp.where(diagonal, row, 0.0), axis=1, keepdims=True)
        affine = affine + column * latb[s][0:1]
    awg_ref[...] = affine
    abg_ref[...] = style_sum[:, :ib]

    for d in range(1, SAMPLES):
        src = lax.rem(b + SAMPLES - d, SAMPLES)
        remote(kg.at[src], kg.at[src], kg_s.at[d], kg_r.at[d], samples=src).wait_recv()

    for kw in range(3):
        each = [kg[s, kw].astype(F32) for s in range(SAMPLES)]
        for k in range(nb):
            total = sum(selb[s][0:1, k : k + 1] * each[s] for s in range(SAMPLES))
            for kh in range(3):
                bg_ref[k, 3 * kh + kw] = total[:, (2 - kh) * ch : (3 - kh) * ch]

    for copy in sent:
        copy.wait_send()
    for part in range(2):
        @pl.when(2 * c + part != r)
        def _():
            remote(gs.at[0, part], gbuf.at[r], g_s.at[0, part], g_r.at[r], rows=2 * c + part).wait_send()

    @pl.when(not_first)
    def _():
        edge(f_ref.at[0], fhalo, fh_s, fh_r, True).wait_send()
        edge(dsend.at[0], dhalo, dh_s, dh_r, True).wait_send()

    @pl.when(not_last)
    def _():
        edge(f_ref.at[0], fhalo, fh_s, fh_r, False).wait_send()
        edge(dsend.at[1], dhalo, dh_s, dh_r, False).wait_send()


def on_device(feature, out_grad, bank, select, latent, affine_w, affine_b):
    x = jnp.transpose(out_grad[0], (1, 0, 2))
    f = jnp.transpose(feature[0], (1, 0, 2))
    height, ch, width = x.shape
    nb, taps, _, ib = bank.shape
    z = latent.shape[1]
    lanes = 4 * ch
    vmem = pl.BlockSpec(memory_space=pltpu.VMEM)
    dma = pltpu.SemaphoreType.DMA
    d, bg, awg, abg = pl.pallas_call(
        kernel,
        out_shape=(
            jax.ShapeDtypeStruct((height, ch, width), BF16),
            jax.ShapeDtypeStruct((nb, taps, ib, ch), F32),
            jax.ShapeDtypeStruct((ib, z), F32),
            jax.ShapeDtypeStruct((1, ib), F32),
        ),
        in_specs=[vmem] * 7,
        out_specs=(vmem,) * 4,
        scratch_shapes=[
            pltpu.VMEM((height + 5, CHANS, ch, width), BF16),
            pltpu.VMEM((height + 2, 3 * ch, width), BF16),
            pltpu.VMEM((2, ch, width), BF16),
            pltpu.VMEM((ROWS, 3, ib, lanes), BF16),
            pltpu.VMEM((CHANS, 2, 3, ib, lanes), BF16),
            pltpu.VMEM((CHANS, 2, 3, ib, lanes), BF16),
            pltpu.VMEM((ROWS, 3, ib, lanes), BF16),
            pltpu.VMEM((SAMPLES, 8, z), F32),
            pltpu.VMEM((SAMPLES, 8, 128), F32),
            pltpu.VMEM((ROWS, 1, 128), F32),
            pltpu.VMEM((ROWS, CHANS, 1, 128), F32),
            pltpu.VMEM((CHANS, 1, 128), F32),
            pltpu.VMEM((SAMPLES, 3, ib, lanes), BF16),
            pltpu.VMEM((SAMPLES, CHANS, 1, 128), F32),
            pltpu.VMEM((3, ib, lanes), F32),
            pltpu.VMEM((3, ib, lanes), F32),
            pltpu.VMEM((height + 2, ch, width), F32),
            pltpu.VMEM((2, ch, width), BF16),
            pltpu.VMEM((2, ch, width), BF16),
            dma((2, 4)), dma((2, 4)),
            dma((2,)), dma((2,)),
            dma((2,)), dma((2,)),
            dma,
            dma((2, SAMPLES)), dma((2, SAMPLES)),
            dma((ROWS,)), dma((ROWS,)),
            dma((4,)), dma((4,)), dma((4,)), dma((8,)), dma((4,)),
            dma((CHANS, 2)), dma((ROWS,)),
            dma((ROWS, CHANS)), dma((ROWS, CHANS)),
            dma((SAMPLES,)), dma((SAMPLES,)),
            dma((SAMPLES, CHANS)), dma((SAMPLES, CHANS)),
        ],
        compiler_params=pltpu.CompilerParams(
            collective_id=0, has_side_effects=True, vmem_limit_bytes=48 * 1024 * 1024
        ),
    )(
        x, f, jnp.transpose(bank, (0, 1, 3, 2)), select, latent,
        jnp.transpose(affine_w), affine_b[None],
    )
    return (
        jnp.transpose(d, (1, 0, 2))[None],
        jnp.transpose(bg, (0, 1, 3, 2)),
        jnp.transpose(awg),
        abg[0],
    )


def solution(mesh):
    return jax.shard_map(
        on_device,
        mesh=mesh,
        in_specs=(
            P("samples", "chan", "rows", None),
            P("samples", "chan", "rows", None),
            P(None, None, "chan", "rows"),
            P("samples", None),
            P("samples", None),
            P(None, "rows"),
            P("rows"),
        ),
        out_specs=(
            P("samples", "chan", "rows", None),
            P(None, None, "chan", "rows"),
            P(None, "rows"),
            P("rows"),
        ),
        check_vma=False,
    )
```

time: 70.9 us -> 56.8 us (0.80)
  Pallas kernels: 64.7 us -> 50.7 us
    pallas_call x1, Pallas kernels: 64.7 us -> 50.7 us  [on_device(): pl.pallas_call(kernel, out_shape=(jax.ShapeDtypeStruct((height, ch, width...]
where the time goes in v2:
time: 56.8 us; the launch traced here: 56.6 us
  Pallas kernels  50.7 us (89%)
  local copies, waits for them, and re-layouts  5.27 us (9%)
  between operations  0.7 us (1%)
    pallas_call x1, Pallas kernels, on_device(): pl.pallas_call(kernel, out_shape=(jax.ShapeDtypeStruct((height, ch, width...  50.7 us
    unnamed x14, local copies, waits for them, and re-layouts  3.69 us
    transpose x1, local copies, waits for them, and re-layouts, on_device(): f = jnp.transpose(feature[0], (1, 0, 2))  1.58 us

profile of v2, /device:TPU:1, one launch (start us, length us, event | category | flops | bytes accessed | tf_op | source)
XLA Modules:
  0.0 56.6 jit_solution(6203480112982797781)
XLA Ops:
  0.6 0.0 copy-start
  0.6 0.0 copy-start.1
  0.7 1.6 %copy_bitcast_fusion = (bf16[8,64,512]{2,1,0:T(8,128)(2,1)S(1)}, bf16[8,64,512]{2,1,0:T(8,128)(2,1)S(1)}) fusion(bf16[1,64,8,512]{3,2,1,0:T(8,128)(2,1)} %param.7, bf16[1,64,8,512]{3,2,1,0:T(8,128)(2,1)} %param.8), kind=kLoop, calls=%fused_computation | loop fusion | bytes 2097152 | tf_op jit(solution)/shard_map/transpose | solution.py:405
  2.2 0.0 copy-start.2
  2.2 0.0 copy-start.3
  2.3 0.0 copy-start.4
  2.3 0.0 copy-done
  2.3 0.0 copy-done.1
  2.3 0.6 %copy-done.2 = f32[1,512]{1,0:T(1,128)S(1)} copy-done((f32[1,512]{1,0:T(1,128)S(1)}, f32[1,512]{1,0:T(1,128)}, u32[]{:S(2)}) %copy-start.2) | copy-done | bytes 2072
  2.9 0.0 copy-done.3
  2.9 0.0 copy-done.4
  2.9 50.7 %shard_map.102 = (bf16[8,64,512]{2,1,0:T(8,128)(2,1)S(1)}, f32[4,9,32,64]{3,2,1,0:T(8,128)S(1)}, f32[32,512]{1,0:T(8,128)S(1)}, f32[1,32]{1,0:T(1,128)S(1)}) custom-call(bf16[8,64,512]{2,1,0:T(8,128)(2,1)S(1)} %get-tuple-element.17.x_ref, bf16[8,64,512]{2,1,0:T(8,128)(2,1)S(1)} %get-tuple-element.16.f_ref, f32[4,9,32,64]{3,2,1,0:T(8,128)S(1)} %bitcast.17, ...), custom_call_target="tpu_custom_call" | custom-call | tf_op jit(solution)/shard_map/pallas_call | solution.py:412
  53.6 1.1 %copy.13 = bf16[1,64,8,512]{3,2,1,0:T(8,128)(2,1)} copy(bf16[1,64,8,512]{3,1,2,0:T(8,128)(2,1)S(1)} %bitcast.19) | data formatting | bytes 1048576
  54.7 0.8 %copy.19 = f32[4,9,64,32]{2,3,1,0:T(8,128)} copy(f32[4,9,64,32]{2,3,1,0:T(8,128)S(1)} %bitcast.18) | data formatting | bytes 589824
  55.5 0.6 %copy.20 = f32[512,32]{0,1:T(8,128)} copy(f32[512,32]{0,1:T(8,128)S(1)} %bitcast.21) | data formatting | bytes 131072
  56.1 0.5 copy.21
Async XLA Ops:
  0.6 1.6 %copy-start = (f32[4,9,64,32]{2,3,1,0:T(8,128)S(1)}, f32[4,9,64,32]{2,3,1,0:T(8,128)}, u32[]{:S(2)}) copy-start(f32[4,9,64,32]{2,3,1,0:T(8,128)} %param.9) | copy-start | bytes 884740
  0.6 1.6 %copy-start.1 = (f32[512,32]{0,1:T(8,128)S(1)}, f32[512,32]{0,1:T(8,128)}, u32[]{:S(2)}) copy-start(f32[512,32]{0,1:T(8,128)} %param.12) | copy-start | bytes 196612
  2.2 0.7 %copy-start.2 = (f32[1,512]{1,0:T(1,128)S(1)}, f32[1,512]{1,0:T(1,128)}, u32[]{:S(2)}) copy-start(f32[1,512]{1,0:T(1,128)} %lat_ref.1) | copy-start | bytes 6148
  2.2 0.7 %copy-start.3 = (s32[1,4]{1,0:T(1,128)S(1)}, s32[1,4]{1,0:T(1,128)}, u32[]{:S(2)}) copy-start(s32[1,4]{1,0:T(1,128)} %sel_ref.1) | copy-start | bytes 52
  2.3 0.7 %copy-start.4 = (f32[32]{0:T(128)S(1)}, f32[32]{0:T(128)}, u32[]{:S(2)}) copy-start(f32[32]{0:T(128)} %param.13) | copy-start | bytes 388

commit v3 on v2

--- a/solution.py
+++ b/solution.py
@@ -33,8 +33,8 @@
 def kernel(
     x_ref, f_ref, bank_ref, sel_ref, lat_ref, aw_ref, ab_ref,
     d_ref, bg_ref, awg_ref, abg_ref,
-    xbuf, fs, fhalo, mr, mm, gs, gbuf, latb, selb, en, slv, slo, kg, st, ker_ref, plain_ref, dacc, dsend, dhalo,
-    ag_s, ag_r, fh_s, fh_r, dh_s, dh_r, own_s, in_s, in_r, en_s, en_r, mz_s, mf_s, my_s, mr_r, my_r,
+    xbuf, fs, fhalo, mown, ms, my, mm, gs, gbuf, latb, selb, en, slv, slo, kg, st, ker_ref, plain_ref, dacc, dsend, dhalo,
+    ag_s, ag_r, fh_s, fh_r, dh_s, dh_r, own_s, in_s, in_r, en_s, en_r, ms_s, ms_r, my_s, my_r, mm_s, mm_r,
     g_s, g_r, sl_s, sl_r, kg_s, kg_r, st_s, st_r,
 ):
     r, b, c = lax.axis_index("rows"), lax.axis_index("samples"), lax.axis_index("chan")
@@ -109,6 +109,7 @@
         return carry
 
     lax.fori_loop(0, height, shifted, 0)
+    gs[...] = jnp.zeros_like(gs)
     for row in (0, 1, height + 2, height + 3, height + 4):
         xbuf[row] = jnp.zeros(xbuf.shape[1:], BF16)
 
@@ -117,7 +118,6 @@
     for d in range(1, ROWS):
         go(remote(en.at[r], en.at[r], en_s.at[d], en_r.at[d], rows=lax.rem(r + d, ROWS)))
     half = height // 2
-    quarter = height // 4
 
     def rows_of(shard, first, count):
         return xbuf.at[pl.ds(first + 2, count), shard]
@@ -154,19 +154,16 @@
     scale = lax.rsqrt(jnp.sum(en[...], axis=0) + EPS)
     scale = jnp.concatenate([scale, scale], axis=1)[None]
 
-    mr[pl.ds(r, 1)] = (plain * scale).astype(BF16)[None]
     side, level = r // 4, lax.rem(r, 4)
-    across = lax.rem(r + 4, ROWS)
-    go(remote(mr.at[r], mr.at[r], mz_s.at[0], mr_r.at[0], rows=across))
-
-    def peer(d):
-        return 4 * side + lax.rem(level + d, 4)
-
-    def far(d):
-        return 4 * (1 - side) + lax.rem(level + d, 4)
-
-    for d in range(1, 4):
-        go(remote(mr.at[r], mr.at[r], mz_s.at[d], mr_r.at[d], rows=peer(d)))
+    tile, lanes = 3 * ib // 2, 128
+    modulated = (plain * scale).astype(BF16).reshape(3 * ib, 4 * ch)
+    for quarter in range(4):
+        top, start = (quarter // 2) * tile, (quarter % 2) * lanes
+        mown[quarter] = modulated[top : top + tile, start : start + lanes]
+    ms[pl.ds(r, 1)] = mown[pl.ds(level, 1)]
+    for d in range(1, ROWS):
+        there = lax.rem(r + d, ROWS)
+        go(remote(mown.at[lax.rem(there, 4)], ms.at[r], ms_s.at[d], ms_r.at[d], rows=there))
 
     @pl.when(not_first)
     def _():
@@ -186,15 +183,19 @@
     def _():
         fs[height + 1] = jnp.zeros(fs.shape[1:], BF16)
 
-    def grad_of(i, shard):
+    def grad_rows(acc, shard, first, count):
         def step(q, acc):
-            around = xbuf[pl.ds(q, 4), shard].reshape(4 * ch, width)
+            around = xbuf[pl.ds(q, 3), shard].reshape(3 * ch, width)
             return acc + lax.dot_general(
                 fs[q], around, (((1,), (1,)), ((), ())), preferred_element_type=F32
             )
 
-        acc = lax.fori_loop(0, height + 2, step, jnp.zeros((tall, 4 * ch), F32))
-        gs[i] = acc.reshape(2, 3, ib, 4 * ch).astype(BF16)
+        return lax.fori_loop(first, first + count, step, acc)
+
+    no_grad = jnp.zeros((tall, 3 * ch), F32)
+
+    def send_grad(i, shard, acc):
+        gs[i, :, :, : 3 * ch] = acc.reshape(2, 3 * ib, 3 * ch).astype(BF16)
         for part in range(2):
             src = gs.at[i, part]
             target = 2 * c + part
@@ -210,11 +211,9 @@
                 go(remote(src, gbuf.at[r], g_s.at[i, part], g_r.at[r], rows=target, chan=shard))
 
     own.wait()
-    remote(mr.at[across], mr.at[across], mz_s.at[0], mr_r.at[0], rows=across).wait_recv()
-    for d in range(1, 4):
-        go(remote(mr.at[across], mr.at[across], mf_s.at[d], mr_r.at[4 + d], rows=peer(d)))
-
-    grad_of(0, c)
+    send_grad(0, c, grad_rows(no_grad, c, 0, height + 2))
+
+    most = half - 1
 
     def from_left(k, first, count, shard):
         return remote(rows_of(shard, first, count), rows_of(shard, first, count), ag_s.at[0, k], ag_r.at[0, k], **to_right)
@@ -223,47 +222,48 @@
         return remote(rows_of(shard, first, count), rows_of(shard, first, count), ag_s.at[1, k], ag_r.at[1, k], **to_left)
 
     from_left(0, 0, half, left).wait_recv()
-    go(from_left(2, 0, quarter, left))
+    go(from_left(2, 0, most, left))
+    go(from_left(3, most, 1, left))
     from_right(0, half, half, right).wait_recv()
-    go(from_right(2, height - quarter, quarter, right))
-
-    for d in range(1, 4):
-        src = peer(4 - d)
-        remote(mr.at[src], mr.at[src], mz_s.at[d], mr_r.at[d], rows=src).wait_recv()
-        src = far(4 - d)
-        remote(mr.at[src], mr.at[src], mf_s.at[d], mr_r.at[4 + d], rows=across).wait_recv()
+    go(from_right(2, half + 1, most, right))
+    go(from_right(3, half, 1, right))
+
+    for d in range(1, ROWS):
+        src = lax.rem(r + ROWS - d, ROWS)
+        remote(mown.at[0], ms.at[src], ms_s.at[d], ms_r.at[d], rows=src).wait_recv()
+    my[pl.ds(c, 1)] = ms[pl.ds(2 * c, 2)][None]
     for d in (1, 3, 2):
         there = lax.rem(c + d, CHANS)
-        go(remote(mr.at[pl.ds(2 * there, 2)], mm.at[c], my_s.at[d], my_r.at[d], chan=there))
-    mine = pltpu.make_async_copy(mr.at[pl.ds(2 * c, 2)], mm.at[c], my_r.at[0])
-    mine.start()
-    go(from_left(3, quarter, quarter, left))
-    go(from_right(3, half, quarter, right))
+        go(remote(ms.at[pl.ds(2 * there, 2)], my.at[c], my_s.at[d], my_r.at[d], chan=there))
 
     from_left(1, half, half, left).wait_recv()
-
-    grad_of(1, left)
-
-    from_right(1, 0, half, right).wait_recv()
-
-    grad_of(2, right)
-
-    from_left(2, 0, quarter, opp).wait_recv()
-    from_right(2, height - quarter, quarter, opp).wait_recv()
-
-    from_left(3, quarter, quarter, opp).wait_recv()
-    from_right(3, half, quarter, opp).wait_recv()
-
-    grad_of(3, opp)
 
     for d in range(1, CHANS):
         src = lax.rem(c + CHANS - d, CHANS)
-        remote(mr.at[pl.ds(0, 2)], mm.at[src], my_s.at[d], my_r.at[d], chan=src).wait_recv()
-    mine.wait()
-
-    for i, (k, shard) in enumerate(((0, c), (3, left), (1, right), (2, opp))):
+        remote(ms.at[pl.ds(0, 2)], my.at[src], my_s.at[d], my_r.at[d], chan=src).wait_recv()
+
+    def quarter_of(level):
+        top = pl.multiple_of((level // 2) * tile, tile)
+        start = pl.multiple_of(lax.rem(level, 2) * lanes, lanes)
+        return mm.at[:, :, pl.ds(top, tile), pl.ds(start, lanes)]
+
+    def peer(d):
+        return 4 * side + lax.rem(level + d, 4)
+
+    mine = pltpu.make_async_copy(my, quarter_of(level), mm_r.at[0])
+    mine.start()
+    for d in (1, 3, 2):
+        go(remote(my, quarter_of(level), mm_s.at[d], mm_r.at[d], rows=peer(d)))
+
+    send_grad(1, left, grad_rows(no_grad, left, 0, height + 2))
+
+    from_right(1, 0, half, right).wait_recv()
+
+    send_grad(2, right, grad_rows(no_grad, right, 0, height + 2))
+
+    def send_slope(i, k, shard):
         parts = gs[i].astype(F32) * mm[shard].astype(F32)
-        slo[i] = over_taps(parts[0] + parts[1])
+        slo[i] = over_taps(parts)
         for d in range(ROWS):
             if k == 0 and d == 0:
                 slv[pl.ds(r, 1), pl.ds(c, 1)] = slo[0][None, None]
@@ -271,6 +271,26 @@
                 go(remote(
                     slo.at[i], slv.at[r, c], sl_s.at[d, k], sl_r.at[d, k], rows=lax.rem(r + d, ROWS), chan=shard
                 ))
+
+    from_left(2, 0, most, opp).wait_recv()
+    from_right(2, half + 1, most, opp).wait_recv()
+
+    acc = grad_rows(no_grad, opp, 0, most)
+    acc = grad_rows(acc, opp, height + 2 - most, most)
+
+    for d in range(1, 4):
+        src = peer(4 - d)
+        remote(my, quarter_of(lax.rem(src, 4)), mm_s.at[d], mm_r.at[d], rows=src).wait_recv()
+    mine.wait()
+    send_slope(0, 0, c)
+    send_slope(1, 3, left)
+    send_slope(2, 1, right)
+
+    from_left(3, most, 1, opp).wait_recv()
+    from_right(3, half, 1, opp).wait_recv()
+
+    send_grad(3, opp, grad_rows(acc, opp, most, height + 2 - 2 * most))
+    send_slope(3, 2, opp)
 
     def rows_out(q, carry):
         total = jnp.zeros((tall, width), F32)
@@ -295,7 +315,7 @@
         edge(dsend.at[1], dhalo, dh_s, dh_r, False).start()
 
     for src in range(ROWS):
-        remote(gs.at[0, 0], gbuf.at[src], g_s.at[0, 0], g_r.at[src], rows=across).wait_recv()
+        remote(gs.at[0, 0], gbuf.at[src], g_s.at[0, 0], g_r.at[src], rows=lax.rem(r + 1, ROWS)).wait_recv()
 
     for d in range(ROWS):
         for k in range(CHANS):
@@ -306,6 +326,7 @@
     grad = gbuf[0].astype(F32)
     for src in range(1, ROWS):
         grad = grad + gbuf[src].astype(F32)
+    grad = grad.reshape(3, ib, 4 * ch)
     slope = jnp.sum(slv[...], axis=(0, 1))
     slope = jnp.concatenate([slope, slope], axis=1)[None]
     plain_grad = grad * scale - plain * (slope * (scale * scale))
@@ -423,10 +444,12 @@
             pltpu.VMEM((height + 5, CHANS, ch, width), BF16),
             pltpu.VMEM((height + 2, 3 * ch, width), BF16),
             pltpu.VMEM((2, ch, width), BF16),
-            pltpu.VMEM((ROWS, 3, ib, lanes), BF16),
-            pltpu.VMEM((CHANS, 2, 3, ib, lanes), BF16),
-            pltpu.VMEM((CHANS, 2, 3, ib, lanes), BF16),
-            pltpu.VMEM((ROWS, 3, ib, lanes), BF16),
+            pltpu.VMEM((4, 3 * ib // 2, 128), BF16),
+            pltpu.VMEM((ROWS, 3 * ib // 2, 128), BF16),
+            pltpu.VMEM((CHANS, 2, 3 * ib // 2, 128), BF16),
+            pltpu.VMEM((CHANS, 2, 3 * ib, lanes), BF16),
+            pltpu.VMEM((CHANS, 2, 3 * ib, lanes), BF16),
+            pltpu.VMEM((ROWS, 3 * ib, lanes), BF16),
             pltpu.VMEM((SAMPLES, 8, z), F32),
             pltpu.VMEM((SAMPLES, 8, 128), F32),
             pltpu.VMEM((ROWS, 1, 128), F32),
@@ -445,7 +468,7 @@
             dma,
             dma((2, SAMPLES)), dma((2, SAMPLES)),
             dma((ROWS,)), dma((ROWS,)),
-            dma((4,)), dma((4,)), dma((4,)), dma((8,)), dma((4,)),
+            dma((ROWS,)), dma((ROWS,)), dma((CHANS,)), dma((CHANS,)), dma((4,)), dma((4,)),
             dma((CHANS, 2)), dma((ROWS,)),
             dma((ROWS, CHANS)), dma((ROWS, CHANS)),
             dma((SAMPLES,)), dma((SAMPLES,)),

time: 56.8 us -> 58.6 us (1.032)
  Pallas kernels: 50.7 us -> 52.5 us
    pallas_call x1, Pallas kernels: 50.7 us -> 52.5 us  [on_device(): pl.pallas_call(kernel, out_shape=(jax.ShapeDtypeStruct((height, ch, width...]
where the time goes in v3:
time: 58.6 us; the launch traced here: 58.4 us
  Pallas kernels  52.5 us (90%)
  local copies, waits for them, and re-layouts  5.27 us (9%)
  between operations  0.7 us (1%)
    pallas_call x1, Pallas kernels, on_device(): pl.pallas_call(kernel, out_shape=(jax.ShapeDtypeStruct((height, ch, width...  52.5 us
    unnamed x14, local copies, waits for them, and re-layouts  3.69 us
    transpose x1, local copies, waits for them, and re-layouts, on_device(): f = jnp.transpose(feature[0], (1, 0, 2))  1.58 us

profile of v3, /device:TPU:1, one launch (start us, length us, event | category | flops | bytes accessed | tf_op | source)
XLA Modules:
  0.0 58.4 jit_solution(11273586978015797687)
XLA Ops:
  0.6 0.0 copy-start
  0.6 0.0 copy-start.1
  0.7 1.6 %copy_bitcast_fusion = (bf16[8,64,512]{2,1,0:T(8,128)(2,1)S(1)}, bf16[8,64,512]{2,1,0:T(8,128)(2,1)S(1)}) fusion(bf16[1,64,8,512]{3,2,1,0:T(8,128)(2,1)} %param.7, bf16[1,64,8,512]{3,2,1,0:T(8,128)(2,1)} %param.8), kind=kLoop, calls=%fused_computation | loop fusion | bytes 2097152 | tf_op jit(solution)/shard_map/transpose | solution.py:426
  2.2 0.0 copy-start.2
  2.2 0.0 copy-start.3
  2.3 0.0 copy-start.4
  2.3 0.0 copy-done
  2.3 0.0 copy-done.1
  2.3 0.6 %copy-done.2 = f32[1,512]{1,0:T(1,128)S(1)} copy-done((f32[1,512]{1,0:T(1,128)S(1)}, f32[1,512]{1,0:T(1,128)}, u32[]{:S(2)}) %copy-start.2) | copy-done | bytes 2072
  2.9 0.0 copy-done.3
  2.9 0.0 copy-done.4
  2.9 52.5 %shard_map.102 = (bf16[8,64,512]{2,1,0:T(8,128)(2,1)S(1)}, f32[4,9,32,64]{3,2,1,0:T(8,128)S(1)}, f32[32,512]{1,0:T(8,128)S(1)}, f32[1,32]{1,0:T(1,128)S(1)}) custom-call(bf16[8,64,512]{2,1,0:T(8,128)(2,1)S(1)} %get-tuple-element.17.x_ref, bf16[8,64,512]{2,1,0:T(8,128)(2,1)S(1)} %get-tuple-element.16.f_ref, f32[4,9,32,64]{3,2,1,0:T(8,128)S(1)} %bitcast.17, ...), custom_call_target="tpu_custom_call" | custom-call | tf_op jit(solution)/shard_map/pallas_call | solution.py:433
  55.4 1.1 %copy.13 = bf16[1,64,8,512]{3,2,1,0:T(8,128)(2,1)} copy(bf16[1,64,8,512]{3,1,2,0:T(8,128)(2,1)S(1)} %bitcast.19) | data formatting | bytes 1048576
  56.5 0.8 %copy.19 = f32[4,9,64,32]{2,3,1,0:T(8,128)} copy(f32[4,9,64,32]{2,3,1,0:T(8,128)S(1)} %bitcast.18) | data formatting | bytes 589824
  57.3 0.6 %copy.20 = f32[512,32]{0,1:T(8,128)} copy(f32[512,32]{0,1:T(8,128)S(1)} %bitcast.21) | data formatting | bytes 131072
  57.9 0.5 copy.21
Async XLA Ops:
  0.6 1.6 %copy-start = (f32[4,9,64,32]{2,3,1,0:T(8,128)S(1)}, f32[4,9,64,32]{2,3,1,0:T(8,128)}, u32[]{:S(2)}) copy-start(f32[4,9,64,32]{2,3,1,0:T(8,128)} %param.9) | copy-start | bytes 884740
  0.6 1.6 %copy-start.1 = (f32[512,32]{0,1:T(8,128)S(1)}, f32[512,32]{0,1:T(8,128)}, u32[]{:S(2)}) copy-start(f32[512,32]{0,1:T(8,128)} %param.12) | copy-start | bytes 196612
  2.2 0.7 %copy-start.2 = (f32[1,512]{1,0:T(1,128)S(1)}, f32[1,512]{1,0:T(1,128)}, u32[]{:S(2)}) copy-start(f32[1,512]{1,0:T(1,128)} %lat_ref.1) | copy-start | bytes 6148
  2.2 0.7 %copy-start.3 = (s32[1,4]{1,0:T(1,128)S(1)}, s32[1,4]{1,0:T(1,128)}, u32[]{:S(2)}) copy-start(s32[1,4]{1,0:T(1,128)} %sel_ref.1) | copy-start | bytes 52
  2.3 0.7 %copy-start.4 = (f32[32]{0:T(128)S(1)}, f32[32]{0:T(128)}, u32[]{:S(2)}) copy-start(f32[32]{0:T(128)} %param.13) | copy-start | bytes 388

commit v4 on v3

--- a/solution.py
+++ b/solution.py
@@ -221,13 +221,6 @@
     def from_right(k, first, count, shard):
         return remote(rows_of(shard, first, count), rows_of(shard, first, count), ag_s.at[1, k], ag_r.at[1, k], **to_left)
 
-    from_left(0, 0, half, left).wait_recv()
-    go(from_left(2, 0, most, left))
-    go(from_left(3, most, 1, left))
-    from_right(0, half, half, right).wait_recv()
-    go(from_right(2, half + 1, most, right))
-    go(from_right(3, half, 1, right))
-
     for d in range(1, ROWS):
         src = lax.rem(r + ROWS - d, ROWS)
         remote(mown.at[0], ms.at[src], ms_s.at[d], ms_r.at[d], rows=src).wait_recv()
@@ -235,6 +228,13 @@
     for d in (1, 3, 2):
         there = lax.rem(c + d, CHANS)
         go(remote(ms.at[pl.ds(2 * there, 2)], my.at[c], my_s.at[d], my_r.at[d], chan=there))
+
+    from_left(0, 0, half, left).wait_recv()
+    go(from_left(2, 0, most, left))
+    go(from_left(3, most, 1, left))
+    from_right(0, half, half, right).wait_recv()
+    go(from_right(2, half + 1, most, right))
+    go(from_right(3, half, 1, right))
 
     from_left(1, half, half, left).wait_recv()
 

time: 58.6 us -> 53.3 us (0.910)
  Pallas kernels: 52.5 us -> 47.1 us
    pallas_call x1, Pallas kernels: 52.5 us -> 47.1 us  [on_device(): pl.pallas_call(kernel, out_shape=(jax.ShapeDtypeStruct((height, ch, width...]
where the time goes in v4:
time: 53.3 us; the launch traced here: 53.1 us
  Pallas kernels  47.1 us (88%)
  local copies, waits for them, and re-layouts  5.27 us (10%)
  between operations  0.7 us (1%)
    pallas_call x1, Pallas kernels, on_device(): pl.pallas_call(kernel, out_shape=(jax.ShapeDtypeStruct((height, ch, width...  47.1 us
    unnamed x14, local copies, waits for them, and re-layouts  3.69 us
    transpose x1, local copies, waits for them, and re-layouts, on_device(): f = jnp.transpose(feature[0], (1, 0, 2))  1.58 us

profile of v4, /device:TPU:1, one launch (start us, length us, event | category | flops | bytes accessed | tf_op | source)
XLA Modules:
  0.0 53.1 jit_solution(11697316355089310776)
XLA Ops:
  0.6 0.0 copy-start
  0.6 0.0 copy-start.1
  0.7 1.6 %copy_bitcast_fusion = (bf16[8,64,512]{2,1,0:T(8,128)(2,1)S(1)}, bf16[8,64,512]{2,1,0:T(8,128)(2,1)S(1)}) fusion(bf16[1,64,8,512]{3,2,1,0:T(8,128)(2,1)} %param.7, bf16[1,64,8,512]{3,2,1,0:T(8,128)(2,1)} %param.8), kind=kLoop, calls=%fused_computation | loop fusion | bytes 2097152 | tf_op jit(solution)/shard_map/transpose | solution.py:426
  2.2 0.0 copy-start.2
  2.2 0.0 copy-start.3
  2.3 0.0 copy-start.4
  2.3 0.0 copy-done
  2.3 0.0 copy-done.1
  2.3 0.6 %copy-done.2 = f32[1,512]{1,0:T(1,128)S(1)} copy-done((f32[1,512]{1,0:T(1,128)S(1)}, f32[1,512]{1,0:T(1,128)}, u32[]{:S(2)}) %copy-start.2) | copy-done | bytes 2072
  2.9 0.0 copy-done.3
  2.9 0.0 copy-done.4
  2.9 47.1 %shard_map.102 = (bf16[8,64,512]{2,1,0:T(8,128)(2,1)S(1)}, f32[4,9,32,64]{3,2,1,0:T(8,128)S(1)}, f32[32,512]{1,0:T(8,128)S(1)}, f32[1,32]{1,0:T(1,128)S(1)}) custom-call(bf16[8,64,512]{2,1,0:T(8,128)(2,1)S(1)} %get-tuple-element.17.x_ref, bf16[8,64,512]{2,1,0:T(8,128)(2,1)S(1)} %get-tuple-element.16.f_ref, f32[4,9,32,64]{3,2,1,0:T(8,128)S(1)} %bitcast.17, ...), custom_call_target="tpu_custom_call" | custom-call | tf_op jit(solution)/shard_map/pallas_call | solution.py:433
  50.1 1.1 %copy.13 = bf16[1,64,8,512]{3,2,1,0:T(8,128)(2,1)} copy(bf16[1,64,8,512]{3,1,2,0:T(8,128)(2,1)S(1)} %bitcast.19) | data formatting | bytes 1048576
  51.2 0.8 %copy.19 = f32[4,9,64,32]{2,3,1,0:T(8,128)} copy(f32[4,9,64,32]{2,3,1,0:T(8,128)S(1)} %bitcast.18) | data formatting | bytes 589824
  52.0 0.6 %copy.20 = f32[512,32]{0,1:T(8,128)} copy(f32[512,32]{0,1:T(8,128)S(1)} %bitcast.21) | data formatting | bytes 131072
  52.6 0.5 copy.21
Async XLA Ops:
  0.6 1.6 %copy-start = (f32[4,9,64,32]{2,3,1,0:T(8,128)S(1)}, f32[4,9,64,32]{2,3,1,0:T(8,128)}, u32[]{:S(2)}) copy-start(f32[4,9,64,32]{2,3,1,0:T(8,128)} %param.9) | copy-start | bytes 884740
  0.6 1.6 %copy-start.1 = (f32[512,32]{0,1:T(8,128)S(1)}, f32[512,32]{0,1:T(8,128)}, u32[]{:S(2)}) copy-start(f32[512,32]{0,1:T(8,128)} %param.12) | copy-start | bytes 196612
  2.2 0.7 %copy-start.2 = (f32[1,512]{1,0:T(1,128)S(1)}, f32[1,512]{1,0:T(1,128)}, u32[]{:S(2)}) copy-start(f32[1,512]{1,0:T(1,128)} %lat_ref.1) | copy-start | bytes 6148
  2.2 0.7 %copy-start.3 = (s32[1,4]{1,0:T(1,128)S(1)}, s32[1,4]{1,0:T(1,128)}, u32[]{:S(2)}) copy-start(s32[1,4]{1,0:T(1,128)} %sel_ref.1) | copy-start | bytes 52
  2.3 0.7 %copy-start.4 = (f32[32]{0:T(128)S(1)}, f32[32]{0:T(128)}, u32[]{:S(2)}) copy-start(f32[32]{0:T(128)} %param.13) | copy-start | bytes 388

commit v5 on v4

--- a/solution.py
+++ b/solution.py
@@ -31,14 +31,14 @@
 
 
 def kernel(
-    x_ref, f_ref, bank_ref, sel_ref, lat_ref, aw_ref, ab_ref,
-    d_ref, bg_ref, awg_ref, abg_ref,
-    xbuf, fs, fhalo, mown, ms, my, mm, gs, gbuf, latb, selb, en, slv, slo, kg, st, ker_ref, plain_ref, dacc, dsend, dhalo,
-    ag_s, ag_r, fh_s, fh_r, dh_s, dh_r, own_s, in_s, in_r, en_s, en_r, ms_s, ms_r, my_s, my_r, mm_s, mm_r,
+    x_hbm, f_hbm, bank_hbm, sel_hbm, lat_hbm, aw_hbm, ab_hbm,
+    d_ref, kg, st, latb, selb,
+    xraw, fraw, f_ref, bank_ref, sel_ref, lat_ref, aw_ref, ab_ref, xbuf, fs, fhalo, mown, ms, my, mm, gs, gbuf, en, slv, slo, ker_ref, plain_ref, dacc, dsend, dhalo,
+    ag_s, ag_r, fh_s, fh_r, dh_s, dh_r, load_s, in_s, in_r, en_s, en_r, ms_s, ms_r, my_s, my_r, mm_s, mm_r,
     g_s, g_r, sl_s, sl_r, kg_s, kg_r, st_s, st_r,
 ):
     r, b, c = lax.axis_index("rows"), lax.axis_index("samples"), lax.axis_index("chan")
-    height, ch, width = x_ref.shape
+    ch, height, width = xraw.shape
     nb, ib = bank_ref.shape[0], bank_ref.shape[2]
     left, right, opp = lax.rem(c + 3, CHANS), lax.rem(c + 1, CHANS), lax.rem(c + 2, CHANS)
     tall = 6 * ib
@@ -74,6 +74,20 @@
             )
             greeted += 1
 
+    pairs = (
+        (lat_hbm, lat_ref), (sel_hbm, sel_ref), (ab_hbm, ab_ref), (aw_hbm, aw_ref), (bank_hbm, bank_ref),
+        (x_hbm, xraw), (f_hbm, fraw),
+    )
+    loads = [pltpu.make_async_copy(src, dst, load_s.at[i]) for i, (src, dst) in enumerate(pairs)]
+    for load in loads:
+        load.start()
+    gs[...] = jnp.zeros_like(gs)
+    ker_ref[...] = jnp.zeros_like(ker_ref)
+    for row in (0, 1, height + 2, height + 3, height + 4):
+        xbuf[row] = jnp.zeros(xbuf.shape[1:], BF16)
+    for load in loads[:5]:
+        load.wait()
+
     lat = lat_ref[...]
     latb[pl.ds(b, 1)] = jnp.broadcast_to(lat[None], (1, 8, lat.shape[1]))
     sel = sel_ref[...].astype(F32)
@@ -84,7 +98,6 @@
     square = lax.broadcasted_iota(jnp.int32, (ib, ib), 0) == lane_iota((ib, ib))
     bias = jnp.sum(jnp.where(square, ab_ref[...], 0.0), axis=1, keepdims=True)
     style = jnp.sum(aw_ref[...] * lat, axis=1, keepdims=True) + bias
-    ker_ref[...] = jnp.zeros_like(ker_ref)
     for kh in range(3):
         for kw in range(3):
             tap = sum(sel[:, k : k + 1] * bank_ref[k, 3 * kh + kw] for k in range(nb))
@@ -94,8 +107,61 @@
     plain = plain_ref[...]
     en[pl.ds(r, 1)] = over_taps(plain * plain)[None]
 
-    own = pltpu.make_async_copy(x_ref, xbuf.at[pl.ds(2, height), c], own_s)
-    own.start()
+    loads[5].wait()
+    group = 16
+
+    def lay_x(g, carry):
+        some = pl.ds(pl.multiple_of(g * group, group), group)
+        xbuf[pl.ds(2, height), pl.ds(c, 1), some] = (
+            jnp.transpose(xraw[some].astype(F32), (1, 0, 2)).astype(BF16)[:, None]
+        )
+        return carry
+
+    lax.fori_loop(0, ch // group, lay_x, 0)
+
+    pl.semaphore_wait(barrier, greeted)
+
+    for d in range(1, ROWS):
+        go(remote(en.at[r], en.at[r], en_s.at[d], en_r.at[d], rows=lax.rem(r + d, ROWS)))
+    half = height // 2
+
+    def rows_of(shard, first, count):
+        return xbuf.at[pl.ds(first + 2, count), shard]
+
+    to_right, to_left = {"chan": right}, {"chan": left}
+    go(remote(rows_of(c, 0, half), rows_of(c, 0, half), ag_s.at[0, 0], ag_r.at[0, 0], **to_right))
+    go(remote(rows_of(c, half, half), rows_of(c, half, half), ag_s.at[1, 0], ag_r.at[1, 0], **to_left))
+
+    go(remote(rows_of(c, half, half), rows_of(c, half, half), ag_s.at[0, 1], ag_r.at[0, 1], **to_right))
+    go(remote(rows_of(c, 0, half), rows_of(c, 0, half), ag_s.at[1, 1], ag_r.at[1, 1], **to_left))
+    for d in range(1, SAMPLES):
+        there = lax.rem(b + d, SAMPLES)
+        go(remote(latb.at[b], latb.at[b], in_s.at[0, d], in_r.at[0, d], samples=there))
+        go(remote(selb.at[b], selb.at[b], in_s.at[1, d], in_r.at[1, d], samples=there))
+
+    loads[6].wait()
+
+    def lay_f(g, carry):
+        some = pl.ds(pl.multiple_of(g * group, group), group)
+        f_ref[:, some] = jnp.transpose(fraw[some].astype(F32), (1, 0, 2)).astype(BF16)
+        return carry
+
+    lax.fori_loop(0, ch // group, lay_f, 0)
+
+    def edge(src, dst, send, recv, up):
+        there = jnp.maximum(r - 1, 0) if up else jnp.minimum(r + 1, ROWS - 1)
+        i = 0 if up else 1
+        return remote(src, dst.at[1 - i], send.at[i], recv.at[1 - i], rows=there)
+
+    not_first, not_last = r > 0, r < ROWS - 1
+
+    @pl.when(not_first)
+    def _():
+        edge(f_ref.at[0], fhalo, fh_s, fh_r, True).start()
+
+    @pl.when(not_last)
+    def _():
+        edge(f_ref.at[height - 1], fhalo, fh_s, fh_r, False).start()
 
     def shift_into(at, f):
         wide = f.astype(F32)
@@ -109,44 +175,6 @@
         return carry
 
     lax.fori_loop(0, height, shifted, 0)
-    gs[...] = jnp.zeros_like(gs)
-    for row in (0, 1, height + 2, height + 3, height + 4):
-        xbuf[row] = jnp.zeros(xbuf.shape[1:], BF16)
-
-    pl.semaphore_wait(barrier, greeted)
-
-    for d in range(1, ROWS):
-        go(remote(en.at[r], en.at[r], en_s.at[d], en_r.at[d], rows=lax.rem(r + d, ROWS)))
-    half = height // 2
-
-    def rows_of(shard, first, count):
-        return xbuf.at[pl.ds(first + 2, count), shard]
-
-    to_right, to_left = {"chan": right}, {"chan": left}
-    go(remote(x_ref.at[pl.ds(0, half)], rows_of(c, 0, half), ag_s.at[0, 0], ag_r.at[0, 0], **to_right))
-    go(remote(x_ref.at[pl.ds(half, half)], rows_of(c, half, half), ag_s.at[1, 0], ag_r.at[1, 0], **to_left))
-
-    def edge(src, dst, send, recv, up):
-        there = jnp.maximum(r - 1, 0) if up else jnp.minimum(r + 1, ROWS - 1)
-        i = 0 if up else 1
-        return remote(src, dst.at[1 - i], send.at[i], recv.at[1 - i], rows=there)
-
-    not_first, not_last = r > 0, r < ROWS - 1
-
-    @pl.when(not_first)
-    def _():
-        edge(f_ref.at[0], fhalo, fh_s, fh_r, True).start()
-
-    @pl.when(not_last)
-    def _():
-        edge(f_ref.at[height - 1], fhalo, fh_s, fh_r, False).start()
-
-    go(remote(x_ref.at[pl.ds(half, half)], rows_of(c, half, half), ag_s.at[0, 1], ag_r.at[0, 1], **to_right))
-    go(remote(x_ref.at[pl.ds(0, half)], rows_of(c, 0, half), ag_s.at[1, 1], ag_r.at[1, 1], **to_left))
-    for d in range(1, SAMPLES):
-        there = lax.rem(b + d, SAMPLES)
-        go(remote(latb.at[b], latb.at[b], in_s.at[0, d], in_r.at[0, d], samples=there))
-        go(remote(selb.at[b], selb.at[b], in_s.at[1, d], in_r.at[1, d], samples=there))
 
     for d in range(1, ROWS):
         src = lax.rem(r + ROWS - d, ROWS)
@@ -210,7 +238,6 @@
             else:
                 go(remote(src, gbuf.at[r], g_s.at[i, part], g_r.at[r], rows=target, chan=shard))
 
-    own.wait()
     send_grad(0, c, grad_rows(no_grad, c, 0, height + 2))
 
     most = half - 1
@@ -348,26 +375,22 @@
     for d in range(1, SAMPLES):
         go(remote(kg.at[b], kg.at[b], kg_s.at[d], kg_r.at[d], samples=lax.rem(b + d, SAMPLES)))
 
-    for h in range(1, height - 1):
-        d_ref[h] = dacc[h + 1].astype(BF16)
-
-    @pl.when(r == 0)
-    def _():
-        d_ref[0] = dacc[1].astype(BF16)
-
     @pl.when(not_first)
     def _():
         edge(dsend.at[0], dhalo, dh_s, dh_r, False).wait_recv()
-        d_ref[0] = (dacc[1] + dhalo[0].astype(F32)).astype(BF16)
-
-    @pl.when(r == ROWS - 1)
-    def _():
-        d_ref[height - 1] = dacc[height].astype(BF16)
+        dacc[1] = dacc[1] + dhalo[0].astype(F32)
 
     @pl.when(not_last)
     def _():
         edge(dsend.at[0], dhalo, dh_s, dh_r, True).wait_recv()
-        d_ref[height - 1] = (dacc[height] + dhalo[1].astype(F32)).astype(BF16)
+        dacc[height] = dacc[height] + dhalo[1].astype(F32)
+
+    def lay_d(g, carry):
+        some = pl.ds(pl.multiple_of(g * group, group), group)
+        d_ref[some] = jnp.transpose(dacc[pl.ds(1, height), some], (1, 0, 2)).astype(BF16)
+        return carry
+
+    lax.fori_loop(0, ch // group, lay_d, 0)
 
     for d in range(1, SAMPLES):
         src = lax.rem(b + SAMPLES - d, SAMPLES)
@@ -381,6 +404,39 @@
                     st.at[bs, cs], st.at[bs, cs], st_s.at[db, dc], st_r.at[db, dc], samples=bs, chan=cs
                 ).wait_recv()
 
+    for d in range(1, SAMPLES):
+        src = lax.rem(b + SAMPLES - d, SAMPLES)
+        remote(kg.at[src], kg.at[src], kg_s.at[d], kg_r.at[d], samples=src).wait_recv()
+
+    for copy in sent:
+        copy.wait_send()
+    for part in range(2):
+        @pl.when(2 * c + part != r)
+        def _():
+            remote(gs.at[0, part], gbuf.at[r], g_s.at[0, part], g_r.at[r], rows=2 * c + part).wait_send()
+
+    @pl.when(not_first)
+    def _():
+        edge(f_ref.at[0], fhalo, fh_s, fh_r, True).wait_send()
+        edge(dsend.at[0], dhalo, dh_s, dh_r, True).wait_send()
+
+    @pl.when(not_last)
+    def _():
+        edge(f_ref.at[0], fhalo, fh_s, fh_r, False).wait_send()
+        edge(dsend.at[1], dhalo, dh_s, dh_r, False).wait_send()
+
+
+def write_out(d_ref, kg, st, latb, selb, d_hbm, bg_hbm, awg_hbm, abg_hbm, bg_ref, awg_ref, abg_ref, sems):
+    nb, _, ib, ch = bg_ref.shape
+    copies = [pltpu.make_async_copy(d_ref, d_hbm, sems.at[0])]
+    copies[0].start()
+    for k in range(nb):
+        for kw in range(3):
+            total = sum(selb[s][0:1, k : k + 1] * kg[s, kw].astype(F32) for s in range(SAMPLES))
+            for kh in range(3):
+                bg_ref[k, 3 * kh + kw] = total[:, (2 - kh) * ch : (3 - kh) * ch]
+        copies.append(pltpu.make_async_copy(bg_ref.at[k], bg_hbm.at[k], sems.at[3 + k]))
+        copies[-1].start()
     diagonal = lax.broadcasted_iota(jnp.int32, (ib, 128), 0) == lane_iota((ib, 128))
     style_sum = jnp.zeros((1, 128), F32)
     affine = jnp.zeros(awg_ref.shape, F32)
@@ -391,56 +447,41 @@
         affine = affine + column * latb[s][0:1]
     awg_ref[...] = affine
     abg_ref[...] = style_sum[:, :ib]
-
-    for d in range(1, SAMPLES):
-        src = lax.rem(b + SAMPLES - d, SAMPLES)
-        remote(kg.at[src], kg.at[src], kg_s.at[d], kg_r.at[d], samples=src).wait_recv()
-
-    for kw in range(3):
-        each = [kg[s, kw].astype(F32) for s in range(SAMPLES)]
-        for k in range(nb):
-            total = sum(selb[s][0:1, k : k + 1] * each[s] for s in range(SAMPLES))
-            for kh in range(3):
-                bg_ref[k, 3 * kh + kw] = total[:, (2 - kh) * ch : (3 - kh) * ch]
-
-    for copy in sent:
-        copy.wait_send()
-    for part in range(2):
-        @pl.when(2 * c + part != r)
-        def _():
-            remote(gs.at[0, part], gbuf.at[r], g_s.at[0, part], g_r.at[r], rows=2 * c + part).wait_send()
-
-    @pl.when(not_first)
-    def _():
-        edge(f_ref.at[0], fhalo, fh_s, fh_r, True).wait_send()
-        edge(dsend.at[0], dhalo, dh_s, dh_r, True).wait_send()
-
-    @pl.when(not_last)
-    def _():
-        edge(f_ref.at[0], fhalo, fh_s, fh_r, False).wait_send()
-        edge(dsend.at[1], dhalo, dh_s, dh_r, False).wait_send()
+    copies.append(pltpu.make_async_copy(awg_ref, awg_hbm, sems.at[1]))
+    copies[-1].start()
+    copies.append(pltpu.make_async_copy(abg_ref, abg_hbm, sems.at[2]))
+    copies[-1].start()
+    for copy in copies:
+        copy.wait()
 
 
 def on_device(feature, out_grad, bank, select, latent, affine_w, affine_b):
-    x = jnp.transpose(out_grad[0], (1, 0, 2))
-    f = jnp.transpose(feature[0], (1, 0, 2))
-    height, ch, width = x.shape
+    _, ch, height, width = out_grad.shape
     nb, taps, _, ib = bank.shape
     z = latent.shape[1]
     lanes = 4 * ch
-    vmem = pl.BlockSpec(memory_space=pltpu.VMEM)
+    vmem, hbm = pl.BlockSpec(memory_space=pltpu.VMEM), pl.BlockSpec(memory_space=pltpu.HBM)
     dma = pltpu.SemaphoreType.DMA
-    d, bg, awg, abg = pl.pallas_call(
+    parts = pl.pallas_call(
         kernel,
         out_shape=(
-            jax.ShapeDtypeStruct((height, ch, width), BF16),
-            jax.ShapeDtypeStruct((nb, taps, ib, ch), F32),
-            jax.ShapeDtypeStruct((ib, z), F32),
-            jax.ShapeDtypeStruct((1, ib), F32),
+            jax.ShapeDtypeStruct((ch, height, width), BF16),
+            jax.ShapeDtypeStruct((SAMPLES, 3, ib, lanes), BF16),
+            jax.ShapeDtypeStruct((SAMPLES, CHANS, 1, 128), F32),
+            jax.ShapeDtypeStruct((SAMPLES, 8, z), F32),
+            jax.ShapeDtypeStruct((SAMPLES, 8, 128), F32),
         ),
-        in_specs=[vmem] * 7,
-        out_specs=(vmem,) * 4,
+        in_specs=[hbm] * 7,
+        out_specs=(vmem,) * 5,
         scratch_shapes=[
+            pltpu.VMEM((ch, height, width), BF16),
+            pltpu.VMEM((ch, height, width), BF16),
+            pltpu.VMEM((height, ch, width), BF16),
+            pltpu.VMEM((nb, taps, ib, ch), F32),
+            pltpu.VMEM((1, nb), jnp.int32),
+            pltpu.VMEM((1, z), F32),
+            pltpu.VMEM((ib, z), F32),
+            pltpu.VMEM((1, ib), F32),
             pltpu.VMEM((height + 5, CHANS, ch, width), BF16),
             pltpu.VMEM((height + 2, 3 * ch, width), BF16),
             pltpu.VMEM((2, ch, width), BF16),
@@ -450,13 +491,9 @@
             pltpu.VMEM((CHANS, 2, 3 * ib, lanes), BF16),
             pltpu.VMEM((CHANS, 2, 3 * ib, lanes), BF16),
             pltpu.VMEM((ROWS, 3 * ib, lanes), BF16),
-            pltpu.VMEM((SAMPLES, 8, z), F32),
-            pltpu.VMEM((SAMPLES, 8, 128), F32),
             pltpu.VMEM((ROWS, 1, 128), F32),
             pltpu.VMEM((ROWS, CHANS, 1, 128), F32),
             pltpu.VMEM((CHANS, 1, 128), F32),
-            pltpu.VMEM((SAMPLES, 3, ib, lanes), BF16),
-            pltpu.VMEM((SAMPLES, CHANS, 1, 128), F32),
             pltpu.VMEM((3, ib, lanes), F32),
             pltpu.VMEM((3, ib, lanes), F32),
             pltpu.VMEM((height + 2, ch, width), F32),
@@ -465,7 +502,7 @@
             dma((2, 4)), dma((2, 4)),
             dma((2,)), dma((2,)),
             dma((2,)), dma((2,)),
-            dma,
+            dma((7,)),
             dma((2, SAMPLES)), dma((2, SAMPLES)),
             dma((ROWS,)), dma((ROWS,)),
             dma((ROWS,)), dma((ROWS,)), dma((CHANS,)), dma((CHANS,)), dma((4,)), dma((4,)),
@@ -478,15 +515,30 @@
             collective_id=0, has_side_effects=True, vmem_limit_bytes=48 * 1024 * 1024
         ),
     )(
-        x, f, jnp.transpose(bank, (0, 1, 3, 2)), select, latent,
-        jnp.transpose(affine_w), affine_b[None],
+        *(pltpu.with_memory_space_constraint(a, pltpu.HBM) for a in (
+            out_grad[0], feature[0], jnp.transpose(bank, (0, 1, 3, 2)), select, latent,
+            jnp.transpose(affine_w), affine_b[None],
+        ))
     )
-    return (
-        jnp.transpose(d, (1, 0, 2))[None],
-        jnp.transpose(bg, (0, 1, 3, 2)),
-        jnp.transpose(awg),
-        abg[0],
-    )
+    d, bg, awg, abg = pl.pallas_call(
+        write_out,
+        out_shape=(
+            jax.ShapeDtypeStruct((ch, height, width), BF16),
+            jax.ShapeDtypeStruct((nb, taps, ib, ch), F32),
+            jax.ShapeDtypeStruct((ib, z), F32),
+            jax.ShapeDtypeStruct((1, ib), F32),
+        ),
+        in_specs=[vmem] * 5,
+        out_specs=(hbm,) * 4,
+        scratch_shapes=[
+            pltpu.VMEM((nb, taps, ib, ch), F32),
+            pltpu.VMEM((ib, z), F32),
+            pltpu.VMEM((1, ib), F32),
+            dma((3 + nb,)),
+        ],
+        compiler_params=pltpu.CompilerParams(vmem_limit_bytes=16 * 1024 * 1024),
+    )(*parts)
+    return d[None], jnp.transpose(bg, (0, 1, 3, 2)), jnp.transpose(awg), abg[0]
 
 
 def solution(mesh):

time: 53.3 us -> 48.9 us (0.917)
  local copies, waits for them, and re-layouts: 5.27 us -> 0 us
  Pallas kernels: 47.1 us -> 48.2 us
    unnamed x14 -> x0, local copies, waits for them, and re-layouts: 3.69 us -> none
    transpose x1 -> x0, local copies, waits for them, and re-layouts: 1.58 us -> none  [on_device(): f = jnp.transpose(feature[0], (1, 0, 2))]
    pallas_call x1 -> x2, Pallas kernels: 47.1 us -> 48.2 us  [the longest x1 47.1 us: on_device(): pl.pallas_call(kernel, out_shape=(jax.ShapeDtypeStruct((ch, height, width...]
where the time goes in v5:
time: 48.9 us; the launch traced here: 48.8 us
  Pallas kernels  48.2 us (99%)
  between operations  0.64 us (1%)
    pallas_call x1, Pallas kernels, on_device(): pl.pallas_call(kernel, out_shape=(jax.ShapeDtypeStruct((ch, height, width...  47.1 us
    pallas_call x1, Pallas kernels, on_device(): pl.pallas_call(write_out, out_shape=(jax.ShapeDtypeStruct((ch, height, wi...  1.09 us

profile of v5, /device:TPU:1, one launch (start us, length us, event | category | flops | bytes accessed | tf_op | source)
XLA Modules:
  0.0 48.8 jit_solution(17918047733033962686)
XLA Ops:
  0.6 47.1 %shard_map.102 = (bf16[64,8,512]{2,1,0:T(8,128)(2,1)S(1)}, bf16[4,3,32,256]{3,2,1,0:T(8,128)(2,1)S(1)}, f32[4,4,1,128]{3,2,1,0:T(1,128)S(1)}, f32[4,8,512]{2,1,0:T(8,128)S(1)}, f32[4,8,128]{2,1,0:T(8,128)S(1)}) custom-call(bf16[64,8,512]{2,1,0:T(8,128)(2,1)} %bitcast.10, bf16[64,8,512]{2,1,0:T(8,128)(2,1)} %bitcast.11, f32[4,9,32,64]{3,2,1,0:T(8,128)} %bitcast.9, ...), custom_call_target="tpu_custom_call" | custom-call | tf_op jit(solution)/shard_map/pallas_call | solution.py:465
  47.7 1.1 %shard_map.103 = (bf16[64,8,512]{2,1,0:T(8,128)(2,1)}, f32[4,9,32,64]{3,2,1,0:T(8,128)}, f32[32,512]{1,0:T(8,128)}, f32[1,32]{1,0:T(1,128)}) custom-call(bf16[64,8,512]{2,1,0:T(8,128)(2,1)S(1)} %get-tuple-element.13.d_ref, bf16[4,3,32,256]{3,2,1,0:T(8,128)(2,1)S(1)} %get-tuple-element.14.kg, f32[4,4,1,128]{3,2,1,0:T(1,128)S(1)} %get-tuple-element.15.st, ...), custom_call_target="tpu_custom_call" | custom-call | tf_op jit(solution)/shard_map/pallas_call | solution.py:523

commit v6 on v5

--- a/solution.py
+++ b/solution.py
@@ -30,11 +30,26 @@
     return half + pltpu.roll(half, 64, axis=1)
 
 
+def packed(x):
+    half = x.shape[0] // 2
+    return jnp.concatenate(
+        [x[:, :128], jnp.concatenate([x[:half, 128:192], x[half:, 128:192]], axis=1)], axis=0
+    )
+
+
+def unpacked(x):
+    third = x.shape[0] // 3
+    tail = x[2 * third :]
+    return jnp.concatenate(
+        [x[: 2 * third], jnp.concatenate([tail, pltpu.roll(tail, 64, axis=1)], axis=0)], axis=1
+    )
+
+
 def kernel(
     x_hbm, f_hbm, bank_hbm, sel_hbm, lat_hbm, aw_hbm, ab_hbm,
     d_ref, kg, st, latb, selb,
-    xraw, fraw, f_ref, bank_ref, sel_ref, lat_ref, aw_ref, ab_ref, xbuf, fs, fhalo, mown, ms, my, mm, gs, gbuf, en, slv, slo, ker_ref, plain_ref, dacc, dsend, dhalo,
-    ag_s, ag_r, fh_s, fh_r, dh_s, dh_r, load_s, in_s, in_r, en_s, en_r, ms_s, ms_r, my_s, my_r, mm_s, mm_r,
+    xraw, fraw, f_ref, bank_ref, sel_ref, lat_ref, aw_ref, ab_ref, xbuf, fs, fhalo, mown, ms, my, mm, mall, gs, gp, gbuf, en, sc, slv, slo, ker_ref, plain_ref, dacc, dsend, dhalo,
+    ag_s, ag_r, fh_s, fh_r, dh_s, dh_r, load_s, in_s, in_r, en_s, en_r, sc_s, sc_r, ms_s, ms_r, my_s, my_r, mm_s, mm_r,
     g_s, g_r, sl_s, sl_r, kg_s, kg_r, st_s, st_r,
 ):
     r, b, c = lax.axis_index("rows"), lax.axis_index("samples"), lax.axis_index("chan")
@@ -53,6 +68,16 @@
     def go(copy):
         copy.start()
         sent.append(copy)
+
+    group = 16
+    pairs = [
+        (lat_hbm, lat_ref), (sel_hbm, sel_ref), (ab_hbm, ab_ref), (aw_hbm, aw_ref), (bank_hbm, bank_ref),
+        *((x_hbm.at[pl.ds(g, group)], xraw.at[pl.ds(g, group)]) for g in range(0, ch, group)),
+        (f_hbm, fraw),
+    ]
+    loads = [pltpu.make_async_copy(src, dst, load_s.at[i]) for i, (src, dst) in enumerate(pairs)]
+    for load in loads:
+        load.start()
 
     barrier = pltpu.get_barrier_semaphore()
     greeted = 0
@@ -74,13 +99,6 @@
             )
             greeted += 1
 
-    pairs = (
-        (lat_hbm, lat_ref), (sel_hbm, sel_ref), (ab_hbm, ab_ref), (aw_hbm, aw_ref), (bank_hbm, bank_ref),
-        (x_hbm, xraw), (f_hbm, fraw),
-    )
-    loads = [pltpu.make_async_copy(src, dst, load_s.at[i]) for i, (src, dst) in enumerate(pairs)]
-    for load in loads:
-        load.start()
     gs[...] = jnp.zeros_like(gs)
     ker_ref[...] = jnp.zeros_like(ker_ref)
     for row in (0, 1, height + 2, height + 3, height + 4):
@@ -107,20 +125,25 @@
     plain = plain_ref[...]
     en[pl.ds(r, 1)] = over_taps(plain * plain)[None]
 
-    loads[5].wait()
-    group = 16
-
-    def lay_x(g, carry):
-        some = pl.ds(pl.multiple_of(g * group, group), group)
-        xbuf[pl.ds(2, height), pl.ds(c, 1), some] = (
-            jnp.transpose(xraw[some].astype(F32), (1, 0, 2)).astype(BF16)[:, None]
+    side, level = r // 4, lax.rem(r, 4)
+    tile, lanes = 3 * ib // 2, 128
+    styled = plain.astype(BF16).reshape(3 * ib, 4 * ch)
+    for quarter in range(4):
+        top, start = (quarter // 2) * tile, (quarter % 2) * lanes
+        mown[quarter] = styled[top : top + tile, start : start + lanes]
+    ms[pl.ds(r, 1)] = mown[pl.ds(level, 1)]
+
+    for g in range(0, ch, group):
+        loads[5 + g // group].wait()
+        xbuf[2 : 2 + height, pl.ds(c, 1), g : g + group] = (
+            jnp.transpose(xraw[g : g + group].astype(F32), (1, 0, 2)).astype(BF16)[:, None]
         )
-        return carry
-
-    lax.fori_loop(0, ch // group, lay_x, 0)
 
     pl.semaphore_wait(barrier, greeted)
 
+    for d in range(1, ROWS):
+        there = lax.rem(r + d, ROWS)
+        go(remote(mown.at[lax.rem(there, 4)], ms.at[r], ms_s.at[d], ms_r.at[d], rows=there))
     for d in range(1, ROWS):
         go(remote(en.at[r], en.at[r], en_s.at[d], en_r.at[d], rows=lax.rem(r + d, ROWS)))
     half = height // 2
@@ -132,14 +155,13 @@
     go(remote(rows_of(c, 0, half), rows_of(c, 0, half), ag_s.at[0, 0], ag_r.at[0, 0], **to_right))
     go(remote(rows_of(c, half, half), rows_of(c, half, half), ag_s.at[1, 0], ag_r.at[1, 0], **to_left))
 
-    go(remote(rows_of(c, half, half), rows_of(c, half, half), ag_s.at[0, 1], ag_r.at[0, 1], **to_right))
-    go(remote(rows_of(c, 0, half), rows_of(c, 0, half), ag_s.at[1, 1], ag_r.at[1, 1], **to_left))
+    most = half - 1
     for d in range(1, SAMPLES):
         there = lax.rem(b + d, SAMPLES)
         go(remote(latb.at[b], latb.at[b], in_s.at[0, d], in_r.at[0, d], samples=there))
         go(remote(selb.at[b], selb.at[b], in_s.at[1, d], in_r.at[1, d], samples=there))
 
-    loads[6].wait()
+    loads[-1].wait()
 
     def lay_f(g, carry):
         some = pl.ds(pl.multiple_of(g * group, group), group)
@@ -175,78 +197,6 @@
         return carry
 
     lax.fori_loop(0, height, shifted, 0)
-
-    for d in range(1, ROWS):
-        src = lax.rem(r + ROWS - d, ROWS)
-        remote(en.at[src], en.at[src], en_s.at[d], en_r.at[d], rows=src).wait_recv()
-    scale = lax.rsqrt(jnp.sum(en[...], axis=0) + EPS)
-    scale = jnp.concatenate([scale, scale], axis=1)[None]
-
-    side, level = r // 4, lax.rem(r, 4)
-    tile, lanes = 3 * ib // 2, 128
-    modulated = (plain * scale).astype(BF16).reshape(3 * ib, 4 * ch)
-    for quarter in range(4):
-        top, start = (quarter // 2) * tile, (quarter % 2) * lanes
-        mown[quarter] = modulated[top : top + tile, start : start + lanes]
-    ms[pl.ds(r, 1)] = mown[pl.ds(level, 1)]
-    for d in range(1, ROWS):
-        there = lax.rem(r + d, ROWS)
-        go(remote(mown.at[lax.rem(there, 4)], ms.at[r], ms_s.at[d], ms_r.at[d], rows=there))
-
-    @pl.when(not_first)
-    def _():
-        edge(f_ref.at[0], fhalo, fh_s, fh_r, False).wait_recv()
-        shift_into(0, fhalo[0])
-
-    @pl.when(r == 0)
-    def _():
-        fs[0] = jnp.zeros(fs.shape[1:], BF16)
-
-    @pl.when(not_last)
-    def _():
-        edge(f_ref.at[0], fhalo, fh_s, fh_r, True).wait_recv()
-        shift_into(height + 1, fhalo[1])
-
-    @pl.when(r == ROWS - 1)
-    def _():
-        fs[height + 1] = jnp.zeros(fs.shape[1:], BF16)
-
-    def grad_rows(acc, shard, first, count):
-        def step(q, acc):
-            around = xbuf[pl.ds(q, 3), shard].reshape(3 * ch, width)
-            return acc + lax.dot_general(
-                fs[q], around, (((1,), (1,)), ((), ())), preferred_element_type=F32
-            )
-
-        return lax.fori_loop(first, first + count, step, acc)
-
-    no_grad = jnp.zeros((tall, 3 * ch), F32)
-
-    def send_grad(i, shard, acc):
-        gs[i, :, :, : 3 * ch] = acc.reshape(2, 3 * ib, 3 * ch).astype(BF16)
-        for part in range(2):
-            src = gs.at[i, part]
-            target = 2 * c + part
-            if i == 0:
-                @pl.when(target == r)
-                def _():
-                    pltpu.make_async_copy(src, gbuf.at[r], g_r.at[r]).start()
-
-                @pl.when(target != r)
-                def _():
-                    remote(src, gbuf.at[r], g_s.at[i, part], g_r.at[r], rows=target).start()
-            else:
-                go(remote(src, gbuf.at[r], g_s.at[i, part], g_r.at[r], rows=target, chan=shard))
-
-    send_grad(0, c, grad_rows(no_grad, c, 0, height + 2))
-
-    most = half - 1
-
-    def from_left(k, first, count, shard):
-        return remote(rows_of(shard, first, count), rows_of(shard, first, count), ag_s.at[0, k], ag_r.at[0, k], **to_right)
-
-    def from_right(k, first, count, shard):
-        return remote(rows_of(shard, first, count), rows_of(shard, first, count), ag_s.at[1, k], ag_r.at[1, k], **to_left)
 
     for d in range(1, ROWS):
         src = lax.rem(r + ROWS - d, ROWS)
@@ -255,6 +205,84 @@
     for d in (1, 3, 2):
         there = lax.rem(c + d, CHANS)
         go(remote(ms.at[pl.ds(2 * there, 2)], my.at[c], my_s.at[d], my_r.at[d], chan=there))
+    go(remote(rows_of(c, half, half), rows_of(c, half, half), ag_s.at[0, 1], ag_r.at[0, 1], **to_right))
+    go(remote(rows_of(c, 0, half), rows_of(c, 0, half), ag_s.at[1, 1], ag_r.at[1, 1], **to_left))
+
+    for d in range(1, ROWS):
+        src = lax.rem(r + ROWS - d, ROWS)
+        remote(en.at[src], en.at[src], en_s.at[d], en_r.at[d], rows=src).wait_recv()
+    scale = lax.rsqrt(jnp.sum(en[...], axis=0) + EPS)
+    sc[pl.ds(c, 1)] = scale[None]
+    for d in range(1, CHANS):
+        go(remote(sc.at[c], sc.at[c], sc_s.at[d], sc_r.at[d], chan=lax.rem(c + d, CHANS)))
+    scale = jnp.concatenate([scale, scale], axis=1)[None]
+
+    @pl.when(not_first)
+    def _():
+        edge(f_ref.at[0], fhalo, fh_s, fh_r, False).wait_recv()
+        shift_into(0, fhalo[0])
+
+    @pl.when(r == 0)
+    def _():
+        fs[0] = jnp.zeros(fs.shape[1:], BF16)
+
+    @pl.when(not_last)
+    def _():
+        edge(f_ref.at[0], fhalo, fh_s, fh_r, True).wait_recv()
+        shift_into(height + 1, fhalo[1])
+
+    @pl.when(r == ROWS - 1)
+    def _():
+        fs[height + 1] = jnp.zeros(fs.shape[1:], BF16)
+
+    def grad_step(acc, shard, q):
+        around = xbuf[q : q + 3, pl.ds(shard, 1)].reshape(3 * ch, width)
+        return acc + lax.dot_general(
+            fs[q], around, (((1,), (1,)), ((), ())), preferred_element_type=F32
+        )
+
+    def grad_rows(acc, shard, steps):
+        for q in steps:
+            acc = grad_step(acc, shard, q)
+        return acc
+
+    no_grad = jnp.zeros((tall, 3 * ch), F32)
+
+    def send_grad(i, shard, acc, slope_first=None):
+        gs[i, :, :, : 3 * ch] = acc.reshape(2, 3 * ib, 3 * ch).astype(BF16)
+        for part in range(2):
+            gp[i, part] = packed(acc[part * 3 * ib : (part + 1) * 3 * ib]).astype(BF16)
+        if slope_first:
+            send_slope(i, *slope_first)
+        for part in range(2):
+            src = gp.at[i, part]
+            target = 2 * c + part
+            if i == 0:
+                @pl.when(target == r)
+                def _():
+                    pltpu.make_async_copy(src, gbuf.at[r], g_r.at[r]).start()
+
+                @pl.when(target != r)
+                def _():
+                    remote(src, gbuf.at[r], g_s.at[i, part], g_r.at[r], rows=target).start()
+            else:
+                go(remote(src, gbuf.at[r], g_s.at[i, part], g_r.at[r], rows=target, chan=shard))
+
+    send_grad(0, c, grad_rows(no_grad, c, range(height + 2)))
+
+    most = half - 1
+
+    def from_left(k, first, count, shard):
+        return remote(rows_of(shard, first, count), rows_of(shard, first, count), ag_s.at[0, k], ag_r.at[0, k], **to_right)
+
+    def from_right(k, first, count, shard):
+        return remote(rows_of(shard, first, count), rows_of(shard, first, count), ag_s.at[1, k], ag_r.at[1, k], **to_left)
+
+    def from_left(k, first, count, shard):
+        return remote(rows_of(shard, first, count), rows_of(shard, first, count), ag_s.at[0, k], ag_r.at[0, k], **to_right)
+
+    def from_right(k, first, count, shard):
+        return remote(rows_of(shard, first, count), rows_of(shard, first, count), ag_s.at[1, k], ag_r.at[1, k], **to_left)
 
     from_left(0, 0, half, left).wait_recv()
     go(from_left(2, 0, most, left))
@@ -263,34 +291,59 @@
     go(from_right(2, half + 1, most, right))
     go(from_right(3, half, 1, right))
 
-    from_left(1, half, half, left).wait_recv()
+    def both_steps(acc_left, acc_right, steps):
+        for q in steps:
+            acc_left = grad_step(acc_left, left, q)
+            acc_right = grad_step(acc_right, right, height + 1 - q)
+        return acc_left, acc_right
+
+    acc_left, acc_right = both_steps(no_grad, no_grad, range(half))
 
     for d in range(1, CHANS):
         src = lax.rem(c + CHANS - d, CHANS)
         remote(ms.at[pl.ds(0, 2)], my.at[src], my_s.at[d], my_r.at[d], chan=src).wait_recv()
 
-    def quarter_of(level):
+    def quarter_of(level, shards=slice(None)):
         top = pl.multiple_of((level // 2) * tile, tile)
         start = pl.multiple_of(lax.rem(level, 2) * lanes, lanes)
-        return mm.at[:, :, pl.ds(top, tile), pl.ds(start, lanes)]
+        return mm.at[shards, :, pl.ds(top, tile), pl.ds(start, lanes)]
 
     def peer(d):
         return 4 * side + lax.rem(level + d, 4)
 
     mine = pltpu.make_async_copy(my, quarter_of(level), mm_r.at[0])
     mine.start()
-    for d in (1, 3, 2):
+    for d in (1, 3):
         go(remote(my, quarter_of(level), mm_s.at[d], mm_r.at[d], rows=peer(d)))
 
-    send_grad(1, left, grad_rows(no_grad, left, 0, height + 2))
-
+    from_left(1, half, half, left).wait_recv()
     from_right(1, 0, half, right).wait_recv()
 
-    send_grad(2, right, grad_rows(no_grad, right, 0, height + 2))
+    acc_left, acc_right = both_steps(acc_left, acc_right, range(half, height + 2))
+    send_grad(1, left, acc_left)
+    send_grad(2, right, acc_right)
+
+    def passed(d, level):
+        part = quarter_of(level, slice(0, 2) if d == 1 else slice(2, 4))
+        return remote(part, part, mm_s.at[1 + d // 2 * 2 + 1], mm_r.at[1 + d // 2 * 2 + 1], rows=peer(d))
+
+    for d in (1, 3):
+        src = lax.rem(level + 4 - d, 4)
+        remote(my, quarter_of(src), mm_s.at[d], mm_r.at[d], rows=peer(4 - d)).wait_recv()
+        go(passed(d, src))
+
+    from_left(2, 0, most, opp).wait_recv()
+    from_right(2, half + 1, most, opp).wait_recv()
+
+    early = list(range(most)) + list(range(height + 2 - most, height + 2))
+    acc_opp = grad_rows(no_grad, opp, early)
+
+    for d in (1, 3):
+        passed(d, lax.rem(level + 2, 4)).wait_recv()
+    mine.wait()
 
     def send_slope(i, k, shard):
-        parts = gs[i].astype(F32) * mm[shard].astype(F32)
-        slo[i] = over_taps(parts)
+        slo[i] = over_taps(gs[i].astype(F32) * mm[shard].astype(F32))
         for d in range(ROWS):
             if k == 0 and d == 0:
                 slv[pl.ds(r, 1), pl.ds(c, 1)] = slo[0][None, None]
@@ -299,16 +352,6 @@
                     slo.at[i], slv.at[r, c], sl_s.at[d, k], sl_r.at[d, k], rows=lax.rem(r + d, ROWS), chan=shard
                 ))
 
-    from_left(2, 0, most, opp).wait_recv()
-    from_right(2, half + 1, most, opp).wait_recv()
-
-    acc = grad_rows(no_grad, opp, 0, most)
-    acc = grad_rows(acc, opp, height + 2 - most, most)
-
-    for d in range(1, 4):
-        src = peer(4 - d)
-        remote(my, quarter_of(lax.rem(src, 4)), mm_s.at[d], mm_r.at[d], rows=src).wait_recv()
-    mine.wait()
     send_slope(0, 0, c)
     send_slope(1, 3, left)
     send_slope(2, 1, right)
@@ -316,20 +359,32 @@
     from_left(3, most, 1, opp).wait_recv()
     from_right(3, half, 1, opp).wait_recv()
 
-    send_grad(3, opp, grad_rows(acc, opp, most, height + 2 - 2 * most))
-    send_slope(3, 2, opp)
-
-    def rows_out(q, carry):
-        total = jnp.zeros((tall, width), F32)
-        for shard in range(CHANS):
-            around = xbuf[pl.ds(q, 4), shard].reshape(4 * ch, width)
-            total = total + jnp.dot(mm[shard].reshape(tall, 4 * ch), around, preferred_element_type=F32)
+    send_grad(3, opp, grad_rows(acc_opp, opp, range(most, height + 2 - most)), slope_first=(2, opp))
+
+    for d in range(1, CHANS):
+        src = lax.rem(c + CHANS - d, CHANS)
+        remote(sc.at[src], sc.at[src], sc_s.at[d], sc_r.at[d], chan=src).wait_recv()
+    for shard in range(CHANS):
+        modulated = mm[shard].reshape(tall, 4 * ch).astype(F32)
+        modulated = (modulated * jnp.concatenate([sc[shard], sc[shard]], axis=1)).astype(BF16)
+        for kh in range(3):
+            at = (kh * CHANS + shard) * ch
+            mall[:, at : at + ch] = modulated[:, kh * ch : (kh + 1) * ch]
+
+    def row_out(q):
+        first, last = max(q, 2), min(q + 3, height + 2)
+        deep = CHANS * ch
+        total = jnp.dot(
+            mall[:, (first - q) * deep : (last - q) * deep],
+            xbuf[first:last].reshape((last - first) * deep, width),
+            preferred_element_type=F32,
+        )
         for part in range(2):
             t = total[3 * part * ib : 3 * (part + 1) * ib]
             dacc[q, part * ib : (part + 1) * ib] = t[ib : 2 * ib] + moved_left(t[:ib]) + moved_right(t[2 * ib :])
-        return carry
-
-    lax.fori_loop(0, height + 2, rows_out, 0)
+
+    row_out(0)
+    row_out(height + 1)
     dsend[0] = dacc[0].astype(BF16)
     dsend[1] = dacc[height + 1].astype(BF16)
 
@@ -341,8 +396,11 @@
     def _():
         edge(dsend.at[1], dhalo, dh_s, dh_r, False).start()
 
+    for q in range(1, height + 1):
+        row_out(q)
+
     for src in range(ROWS):
-        remote(gs.at[0, 0], gbuf.at[src], g_s.at[0, 0], g_r.at[src], rows=lax.rem(r + 1, ROWS)).wait_recv()
+        remote(gp.at[0, 0], gbuf.at[src], g_s.at[0, 0], g_r.at[src], rows=lax.rem(r + 1, ROWS)).wait_recv()
 
     for d in range(ROWS):
         for k in range(CHANS):
@@ -353,10 +411,10 @@
     grad = gbuf[0].astype(F32)
     for src in range(1, ROWS):
         grad = grad + gbuf[src].astype(F32)
-    grad = grad.reshape(3, ib, 4 * ch)
+    grad = unpacked(grad).reshape(3, ib, 4 * ch)
     slope = jnp.sum(slv[...], axis=(0, 1))
     slope = jnp.concatenate([slope, slope], axis=1)[None]
-    plain_grad = grad * scale - plain * (slope * (scale * scale))
+    plain_grad = grad * scale - plain * (slope * (scale * scale * scale))
     by_input = jnp.sum(plain_grad * ker, axis=0)
     by_input = jnp.concatenate([by_input, jnp.zeros((128 - ib, by_input.shape[1]), F32)], axis=0)
     style_part = lax.dot_general(
@@ -371,7 +429,7 @@
                     st.at[b, c], st.at[b, c], st_s.at[db, dc], st_r.at[db, dc],
                     samples=lax.rem(b + db, SAMPLES), chan=lax.rem(c + dc, CHANS),
                 ))
-    kg[pl.ds(b, 1)] = (plain_grad * style[None])[None].astype(BF16)
+    kg[pl.ds(b, 1)] = packed((plain_grad * style[None]).reshape(3 * ib, 4 * ch))[None].astype(BF16)
     for d in range(1, SAMPLES):
         go(remote(kg.at[b], kg.at[b], kg_s.at[d], kg_r.at[d], samples=lax.rem(b + d, SAMPLES)))
 
@@ -413,7 +471,7 @@
     for part in range(2):
         @pl.when(2 * c + part != r)
         def _():
-            remote(gs.at[0, part], gbuf.at[r], g_s.at[0, part], g_r.at[r], rows=2 * c + part).wait_send()
+            remote(gp.at[0, part], gbuf.at[r], g_s.at[0, part], g_r.at[r], rows=2 * c + part).wait_send()
 
     @pl.when(not_first)
     def _():
@@ -428,14 +486,19 @@
 
 def write_out(d_ref, kg, st, latb, selb, d_hbm, bg_hbm, awg_hbm, abg_hbm, bg_ref, awg_ref, abg_ref, sems):
     nb, _, ib, ch = bg_ref.shape
-    copies = [pltpu.make_async_copy(d_ref, d_hbm, sems.at[0])]
-    copies[0].start()
+    quarter = d_ref.shape[0] // 4
+    copies = []
+    for i in range(4):
+        some = pl.ds(i * quarter, quarter)
+        copies.append(pltpu.make_async_copy(d_ref.at[some], d_hbm.at[some], sems.at[2 + nb + i]))
+        copies[-1].start()
+    each = [kg[s].astype(F32) for s in range(SAMPLES)]
     for k in range(nb):
+        total = unpacked(sum(selb[s][0:1, k : k + 1] * each[s] for s in range(SAMPLES)))
         for kw in range(3):
-            total = sum(selb[s][0:1, k : k + 1] * kg[s, kw].astype(F32) for s in range(SAMPLES))
             for kh in range(3):
-                bg_ref[k, 3 * kh + kw] = total[:, (2 - kh) * ch : (3 - kh) * ch]
-        copies.append(pltpu.make_async_copy(bg_ref.at[k], bg_hbm.at[k], sems.at[3 + k]))
+                bg_ref[k, 3 * kh + kw] = total[kw * ib : (kw + 1) * ib, (2 - kh) * ch : (3 - kh) * ch]
+        copies.append(pltpu.make_async_copy(bg_ref.at[k], bg_hbm.at[k], sems.at[2 + k]))
         copies[-1].start()
     diagonal = lax.broadcasted_iota(jnp.int32, (ib, 128), 0) == lane_iota((ib, 128))
     style_sum = jnp.zeros((1, 128), F32)
@@ -447,9 +510,9 @@
         affine = affine + column * latb[s][0:1]
     awg_ref[...] = affine
     abg_ref[...] = style_sum[:, :ib]
-    copies.append(pltpu.make_async_copy(awg_ref, awg_hbm, sems.at[1]))
+    copies.append(pltpu.make_async_copy(awg_ref, awg_hbm, sems.at[0]))
     copies[-1].start()
-    copies.append(pltpu.make_async_copy(abg_ref, abg_hbm, sems.at[2]))
+    copies.append(pltpu.make_async_copy(abg_ref, abg_hbm, sems.at[1]))
     copies[-1].start()
     for copy in copies:
         copy.wait()
@@ -466,7 +529,7 @@
         kernel,
         out_shape=(
             jax.ShapeDtypeStruct((ch, height, width), BF16),
-            jax.ShapeDtypeStruct((SAMPLES, 3, ib, lanes), BF16),
+            jax.ShapeDtypeStruct((SAMPLES, 9 * ib // 2, 128), BF16),
             jax.ShapeDtypeStruct((SAMPLES, CHANS, 1, 128), F32),
             jax.ShapeDtypeStruct((SAMPLES, 8, z), F32),
             jax.ShapeDtypeStruct((SAMPLES, 8, 128), F32),
@@ -489,9 +552,12 @@
             pltpu.VMEM((ROWS, 3 * ib // 2, 128), BF16),
             pltpu.VMEM((CHANS, 2, 3 * ib // 2, 128), BF16),
             pltpu.VMEM((CHANS, 2, 3 * ib, lanes), BF16),
+            pltpu.VMEM((6 * ib, 3 * CHANS * ch), BF16),
             pltpu.VMEM((CHANS, 2, 3 * ib, lanes), BF16),
-            pltpu.VMEM((ROWS, 3 * ib, lanes), BF16),
+            pltpu.VMEM((CHANS, 2, 9 * ib // 2, 128), BF16),
+            pltpu.VMEM((ROWS, 9 * ib // 2, 128), BF16),
             pltpu.VMEM((ROWS, 1, 128), F32),
+            pltpu.VMEM((CHANS, 1, 128), F32),
             pltpu.VMEM((ROWS, CHANS, 1, 128), F32),
             pltpu.VMEM((CHANS, 1, 128), F32),
             pltpu.VMEM((3, ib, lanes), F32),
@@ -499,13 +565,14 @@
             pltpu.VMEM((height + 2, ch, width), F32),
             pltpu.VMEM((2, ch, width), BF16),
             pltpu.VMEM((2, ch, width), BF16),
-            dma((2, 4)), dma((2, 4)),
+            dma((2, 5)), dma((2, 5)),
             dma((2,)), dma((2,)),
             dma((2,)), dma((2,)),
-            dma((7,)),
+            dma((6 + ch // 16,)),
             dma((2, SAMPLES)), dma((2, SAMPLES)),
             dma((ROWS,)), dma((ROWS,)),
-            dma((ROWS,)), dma((ROWS,)), dma((CHANS,)), dma((CHANS,)), dma((4,)), dma((4,)),
+            dma((CHANS,)), dma((CHANS,)),
+            dma((ROWS,)), dma((ROWS,)), dma((CHANS,)), dma((CHANS,)), dma((5,)), dma((5,)),
             dma((CHANS, 2)), dma((ROWS,)),
             dma((ROWS, CHANS)), dma((ROWS, CHANS)),
             dma((SAMPLES,)), dma((SAMPLES,)),
@@ -534,7 +601,7 @@
             pltpu.VMEM((nb, taps, ib, ch), F32),
             pltpu.VMEM((ib, z), F32),
             pltpu.VMEM((1, ib), F32),
-            dma((3 + nb,)),
+            dma((6 + nb,)),
         ],
         compiler_params=pltpu.CompilerParams(vmem_limit_bytes=16 * 1024 * 1024),
     )(*parts)

time: 48.9 us -> 45.8 us (0.937)
  Pallas kernels: 48.2 us -> 45 us
    pallas_call x1, Pallas kernels: 47.1 us -> 43.9 us  [on_device(): pl.pallas_call(kernel, out_shape=(jax.ShapeDtypeStruct((ch, height, width...]
where the time goes in v6:
time: 45.8 us; the launch traced here: 45.6 us
  Pallas kernels  45 us (98%)
  between operations  0.64 us (1%)
    pallas_call x1, Pallas kernels, on_device(): pl.pallas_call(kernel, out_shape=(jax.ShapeDtypeStruct((ch, height, width...  43.9 us
    pallas_call x1, Pallas kernels, on_device(): pl.pallas_call(write_out, out_shape=(jax.ShapeDtypeStruct((ch, height, wi...  1.09 us

profile of v6, /device:TPU:1, one launch (start us, length us, event | category | flops | bytes accessed | tf_op | source)
XLA Modules:
  0.0 45.6 jit_solution(9197898941013152443)
XLA Ops:
  0.6 43.9 %shard_map.102 = (bf16[64,8,512]{2,1,0:T(8,128)(2,1)S(1)}, bf16[4,144,128]{2,1,0:T(8,128)(2,1)S(1)}, f32[4,4,1,128]{3,2,1,0:T(1,128)S(1)}, f32[4,8,512]{2,1,0:T(8,128)S(1)}, f32[4,8,128]{2,1,0:T(8,128)S(1)}) custom-call(bf16[64,8,512]{2,1,0:T(8,128)(2,1)} %bitcast.10, bf16[64,8,512]{2,1,0:T(8,128)(2,1)} %bitcast.11, f32[4,9,32,64]{3,2,1,0:T(8,128)} %bitcast.9, ...), custom_call_target="tpu_custom_call" | custom-call | tf_op jit(solution)/shard_map/pallas_call | solution.py:528
  44.5 1.1 %shard_map.103 = (bf16[64,8,512]{2,1,0:T(8,128)(2,1)}, f32[4,9,32,64]{3,2,1,0:T(8,128)}, f32[32,512]{1,0:T(8,128)}, f32[1,32]{1,0:T(1,128)}) custom-call(bf16[64,8,512]{2,1,0:T(8,128)(2,1)S(1)} %get-tuple-element.13.d_ref, bf16[4,144,128]{2,1,0:T(8,128)(2,1)S(1)} %get-tuple-element.14.kg, f32[4,4,1,128]{3,2,1,0:T(1,128)S(1)} %get-tuple-element.15.st, ...), custom_call_target="tpu_custom_call" | custom-call | tf_op jit(solution)/shard_map/pallas_call | solution.py:590

commit v7 on v6

--- a/solution.py
+++ b/solution.py
@@ -9,6 +9,7 @@
 MESH = pl.DeviceIdType.MESH
 ROWS, SAMPLES, CHANS = 8, 4, 4
 F32, BF16 = jnp.float32, jnp.bfloat16
+FAR_ROWS, FAR_SAMPLES, FAR_CHANS = (2, 6, 3, 5, 1, 7, 4), (2, 3, 1), (2, 1, 3)
 
 
 def lane_iota(shape):
@@ -48,9 +49,9 @@
 def kernel(
     x_hbm, f_hbm, bank_hbm, sel_hbm, lat_hbm, aw_hbm, ab_hbm,
     d_ref, kg, st, latb, selb,
-    xraw, fraw, f_ref, bank_ref, sel_ref, lat_ref, aw_ref, ab_ref, xbuf, fs, fhalo, mown, ms, my, mm, mall, gs, gp, gbuf, en, sc, slv, slo, ker_ref, plain_ref, dacc, dsend, dhalo,
+    xraw, fraw, f_ref, bank_ref, sel_ref, lat_ref, aw_ref, ab_ref, xbuf, fs, fhalo, mown, ms, my, mm, mall, gs, gp, gw, gx, gk, gbuf, en, sc, slv, slo, ker_ref, plain_ref, dacc, dsend, dhalo,
     ag_s, ag_r, fh_s, fh_r, dh_s, dh_r, load_s, in_s, in_r, en_s, en_r, sc_s, sc_r, ms_s, ms_r, my_s, my_r, mm_s, mm_r,
-    g_s, g_r, sl_s, sl_r, kg_s, kg_r, st_s, st_r,
+    gx_s, gx_r, g_s, gf_s, g_r, sl_s, sl_r, kg_s, kg_r, st_s, st_r,
 ):
     r, b, c = lax.axis_index("rows"), lax.axis_index("samples"), lax.axis_index("chan")
     ch, height, width = xraw.shape
@@ -81,8 +82,8 @@
 
     barrier = pltpu.get_barrier_semaphore()
     greeted = 0
-    for dr in range(ROWS):
-        for dc in range(CHANS):
+    for dc in (*FAR_CHANS, 0):
+        for dr in (*FAR_ROWS, 0):
             if dr or dc:
                 pl.semaphore_signal(
                     barrier, inc=1,
@@ -90,8 +91,8 @@
                     device_id_type=MESH,
                 )
                 greeted += 1
-    for db in range(1, SAMPLES):
-        for dc in range(CHANS):
+    for db in FAR_SAMPLES:
+        for dc in (*FAR_CHANS, 0):
             pl.semaphore_signal(
                 barrier, inc=1,
                 device_id={"samples": lax.rem(b + db, SAMPLES), "chan": lax.rem(c + dc, CHANS)},
@@ -100,6 +101,7 @@
             greeted += 1
 
     gs[...] = jnp.zeros_like(gs)
+    gbuf[ROWS // 2 :] = jnp.zeros((ROWS // 2, *gbuf.shape[1:]), BF16)
     ker_ref[...] = jnp.zeros_like(ker_ref)
     for row in (0, 1, height + 2, height + 3, height + 4):
         xbuf[row] = jnp.zeros(xbuf.shape[1:], BF16)
@@ -141,10 +143,10 @@
 
     pl.semaphore_wait(barrier, greeted)
 
-    for d in range(1, ROWS):
+    for d in FAR_ROWS:
         there = lax.rem(r + d, ROWS)
         go(remote(mown.at[lax.rem(there, 4)], ms.at[r], ms_s.at[d], ms_r.at[d], rows=there))
-    for d in range(1, ROWS):
+    for d in FAR_ROWS:
         go(remote(en.at[r], en.at[r], en_s.at[d], en_r.at[d], rows=lax.rem(r + d, ROWS)))
     half = height // 2
 
@@ -156,6 +158,8 @@
     go(remote(rows_of(c, half, half), rows_of(c, half, half), ag_s.at[1, 0], ag_r.at[1, 0], **to_left))
 
     most = half - 1
+    go(remote(rows_of(c, half, 1), rows_of(c, half, 1), ag_s.at[0, 4], ag_r.at[0, 4], **to_right))
+    go(remote(rows_of(c, most, 1), rows_of(c, most, 1), ag_s.at[1, 4], ag_r.at[1, 4], **to_left))
     for d in range(1, SAMPLES):
         there = lax.rem(b + d, SAMPLES)
         go(remote(latb.at[b], latb.at[b], in_s.at[0, d], in_r.at[0, d], samples=there))
@@ -205,8 +209,8 @@
     for d in (1, 3, 2):
         there = lax.rem(c + d, CHANS)
         go(remote(ms.at[pl.ds(2 * there, 2)], my.at[c], my_s.at[d], my_r.at[d], chan=there))
-    go(remote(rows_of(c, half, half), rows_of(c, half, half), ag_s.at[0, 1], ag_r.at[0, 1], **to_right))
-    go(remote(rows_of(c, 0, half), rows_of(c, 0, half), ag_s.at[1, 1], ag_r.at[1, 1], **to_left))
+    go(remote(rows_of(c, half + 1, most), rows_of(c, half + 1, most), ag_s.at[0, 1], ag_r.at[0, 1], **to_right))
+    go(remote(rows_of(c, 0, most), rows_of(c, 0, most), ag_s.at[1, 1], ag_r.at[1, 1], **to_left))
 
     for d in range(1, ROWS):
         src = lax.rem(r + ROWS - d, ROWS)
@@ -248,27 +252,39 @@
 
     no_grad = jnp.zeros((tall, 3 * ch), F32)
 
-    def send_grad(i, shard, acc, slope_first=None):
+    keep = lax.rem(r, 2)
+    partner = r + 1 - 2 * keep
+
+    def swap(i):
+        return remote(gp.at[i, 1 - keep], gx.at[i], gx_s.at[i], gx_r.at[i], rows=partner)
+
+    def send_grad(i, acc):
         gs[i, :, :, : 3 * ch] = acc.reshape(2, 3 * ib, 3 * ch).astype(BF16)
         for part in range(2):
-            gp[i, part] = packed(acc[part * 3 * ib : (part + 1) * 3 * ib]).astype(BF16)
-        if slope_first:
-            send_slope(i, *slope_first)
-        for part in range(2):
-            src = gp.at[i, part]
-            target = 2 * c + part
-            if i == 0:
-                @pl.when(target == r)
-                def _():
-                    pltpu.make_async_copy(src, gbuf.at[r], g_r.at[r]).start()
-
-                @pl.when(target != r)
-                def _():
-                    remote(src, gbuf.at[r], g_s.at[i, part], g_r.at[r], rows=target).start()
-            else:
-                go(remote(src, gbuf.at[r], g_s.at[i, part], g_r.at[r], rows=target, chan=shard))
-
-    send_grad(0, c, grad_rows(no_grad, c, range(height + 2)))
+            wide = packed(acc[part * 3 * ib : (part + 1) * 3 * ib])
+            gw[i, part] = wide
+            gp[i, part] = wide.astype(BF16)
+        if i < 3:
+            go(swap(i))
+
+    def block(i, shard):
+        return remote(gk.at[i], gbuf.at[r // 2], g_s.at[i], g_r.at[r // 2], rows=2 * c + keep, chan=shard)
+
+    def send_block(i, shard):
+        swap(i).wait_recv()
+        gk[i] = (gw[i, keep] + gx[i].astype(F32)).astype(BF16)
+        if i == 0:
+            @pl.when(r // 2 == c)
+            def _():
+                pltpu.make_async_copy(gk.at[0], gbuf.at[r // 2], g_r.at[r // 2]).start()
+
+            @pl.when(r // 2 != c)
+            def _():
+                block(0, c).start()
+        else:
+            go(block(i, shard))
+
+    send_grad(0, grad_rows(no_grad, c, range(height + 2)))
 
     most = half - 1
 
@@ -299,6 +315,8 @@
 
     acc_left, acc_right = both_steps(no_grad, no_grad, range(half))
 
+    send_block(0, c)
+
     for d in range(1, CHANS):
         src = lax.rem(c + CHANS - d, CHANS)
         remote(ms.at[pl.ds(0, 2)], my.at[src], my_s.at[d], my_r.at[d], chan=src).wait_recv()
@@ -316,12 +334,14 @@
     for d in (1, 3):
         go(remote(my, quarter_of(level), mm_s.at[d], mm_r.at[d], rows=peer(d)))
 
-    from_left(1, half, half, left).wait_recv()
-    from_right(1, 0, half, right).wait_recv()
+    from_left(4, half, 1, left).wait_recv()
+    from_right(4, most, 1, right).wait_recv()
+    from_left(1, half + 1, most, left).wait_recv()
+    from_right(1, 0, most, right).wait_recv()
 
     acc_left, acc_right = both_steps(acc_left, acc_right, range(half, height + 2))
-    send_grad(1, left, acc_left)
-    send_grad(2, right, acc_right)
+    send_grad(1, acc_left)
+    send_grad(2, acc_right)
 
     def passed(d, level):
         part = quarter_of(level, slice(0, 2) if d == 1 else slice(2, 4))
@@ -338,13 +358,16 @@
     early = list(range(most)) + list(range(height + 2 - most, height + 2))
     acc_opp = grad_rows(no_grad, opp, early)
 
+    send_block(1, left)
+    send_block(2, right)
+
     for d in (1, 3):
         passed(d, lax.rem(level + 2, 4)).wait_recv()
     mine.wait()
 
     def send_slope(i, k, shard):
         slo[i] = over_taps(gs[i].astype(F32) * mm[shard].astype(F32))
-        for d in range(ROWS):
+        for d in (*FAR_ROWS, 0):
             if k == 0 and d == 0:
                 slv[pl.ds(r, 1), pl.ds(c, 1)] = slo[0][None, None]
             else:
@@ -359,7 +382,10 @@
     from_left(3, most, 1, opp).wait_recv()
     from_right(3, half, 1, opp).wait_recv()
 
-    send_grad(3, opp, grad_rows(acc_opp, opp, range(most, height + 2 - most)), slope_first=(2, opp))
+    send_grad(3, grad_rows(acc_opp, opp, range(most, height + 2 - most)))
+    for part in range(2):
+        go(remote(gp.at[3, part], gbuf.at[r], gf_s.at[part], g_r.at[r], rows=2 * c + part, chan=opp))
+    send_slope(3, 2, opp)
 
     for d in range(1, CHANS):
         src = lax.rem(c + CHANS - d, CHANS)
@@ -399,8 +425,13 @@
     for q in range(1, height + 1):
         row_out(q)
 
-    for src in range(ROWS):
-        remote(gp.at[0, 0], gbuf.at[src], g_s.at[0, 0], g_r.at[src], rows=lax.rem(r + 1, ROWS)).wait_recv()
+    for src in range(ROWS // 2):
+        remote(gk.at[0], gbuf.at[src], g_s.at[0], g_r.at[src], rows=partner).wait_recv()
+
+    @pl.when(lax.rem(c + CHANS - r // 2, CHANS) == 2)
+    def _():
+        for src in range(ROWS // 2, ROWS):
+            remote(gk.at[0], gbuf.at[src], g_s.at[0], g_r.at[src], rows=partner).wait_recv()
 
     for d in range(ROWS):
         for k in range(CHANS):
@@ -422,15 +453,15 @@
         preferred_element_type=F32, precision=lax.Precision.HIGHEST,
     )
     st[pl.ds(b, 1), pl.ds(c, 1)] = style_part[0:1][None, None]
-    for db in range(SAMPLES):
-        for dc in range(CHANS):
+    for dc in (*FAR_CHANS, 0):
+        for db in (*FAR_SAMPLES, 0):
             if db or dc:
                 go(remote(
                     st.at[b, c], st.at[b, c], st_s.at[db, dc], st_r.at[db, dc],
                     samples=lax.rem(b + db, SAMPLES), chan=lax.rem(c + dc, CHANS),
                 ))
     kg[pl.ds(b, 1)] = packed((plain_grad * style[None]).reshape(3 * ib, 4 * ch))[None].astype(BF16)
-    for d in range(1, SAMPLES):
+    for d in FAR_SAMPLES:
         go(remote(kg.at[b], kg.at[b], kg_s.at[d], kg_r.at[d], samples=lax.rem(b + d, SAMPLES)))
 
     @pl.when(not_first)
@@ -468,10 +499,10 @@
 
     for copy in sent:
         copy.wait_send()
-    for part in range(2):
-        @pl.when(2 * c + part != r)
-        def _():
-            remote(gp.at[0, part], gbuf.at[r], g_s.at[0, part], g_r.at[r], rows=2 * c + part).wait_send()
+
+    @pl.when(r // 2 != c)
+    def _():
+        block(0, c).wait_send()
 
     @pl.when(not_first)
     def _():
@@ -555,6 +586,9 @@
             pltpu.VMEM((6 * ib, 3 * CHANS * ch), BF16),
             pltpu.VMEM((CHANS, 2, 3 * ib, lanes), BF16),
             pltpu.VMEM((CHANS, 2, 9 * ib // 2, 128), BF16),
+            pltpu.VMEM((CHANS, 2, 9 * ib // 2, 128), F32),
+            pltpu.VMEM((CHANS, 9 * ib // 2, 128), BF16),
+            pltpu.VMEM((CHANS, 9 * ib // 2, 128), BF16),
             pltpu.VMEM((ROWS, 9 * ib // 2, 128), BF16),
             pltpu.VMEM((ROWS, 1, 128), F32),
             pltpu.VMEM((CHANS, 1, 128), F32),
@@ -573,7 +607,7 @@
             dma((ROWS,)), dma((ROWS,)),
             dma((CHANS,)), dma((CHANS,)),
             dma((ROWS,)), dma((ROWS,)), dma((CHANS,)), dma((CHANS,)), dma((5,)), dma((5,)),
-            dma((CHANS, 2)), dma((ROWS,)),
+            dma((CHANS,)), dma((CHANS,)), dma((CHANS,)), dma((2,)), dma((ROWS,)),
             dma((ROWS, CHANS)), dma((ROWS, CHANS)),
             dma((SAMPLES,)), dma((SAMPLES,)),
             dma((SAMPLES, CHANS)), dma((SAMPLES, CHANS)),

time: 45.8 us -> 45 us (0.983)
  Pallas kernels: 45 us -> 44.2 us
    pallas_call x1, Pallas kernels: 43.9 us -> 43.1 us  [on_device(): pl.pallas_call(kernel, out_shape=(jax.ShapeDtypeStruct((ch, height, width...]
where the time goes in v7:
time: 45 us; the launch traced here: 44.8 us
  Pallas kernels  44.2 us (98%)
  between operations  0.64 us (1%)
    pallas_call x1, Pallas kernels, on_device(): pl.pallas_call(kernel, out_shape=(jax.ShapeDtypeStruct((ch, height, width...  43.1 us
    pallas_call x1, Pallas kernels, on_device(): pl.pallas_call(write_out, out_shape=(jax.ShapeDtypeStruct((ch, height, wi...  1.09 us

profile of v7, /device:TPU:1, one launch (start us, length us, event | category | flops | bytes accessed | tf_op | source)
XLA Modules:
  0.0 44.8 jit_solution(15711791285008162172)
XLA Ops:
  0.6 43.1 %shard_map.102 = (bf16[64,8,512]{2,1,0:T(8,128)(2,1)S(1)}, bf16[4,144,128]{2,1,0:T(8,128)(2,1)S(1)}, f32[4,4,1,128]{3,2,1,0:T(1,128)S(1)}, f32[4,8,512]{2,1,0:T(8,128)S(1)}, f32[4,8,128]{2,1,0:T(8,128)S(1)}) custom-call(bf16[64,8,512]{2,1,0:T(8,128)(2,1)} %bitcast.10, bf16[64,8,512]{2,1,0:T(8,128)(2,1)} %bitcast.11, f32[4,9,32,64]{3,2,1,0:T(8,128)} %bitcast.9, ...), custom_call_target="tpu_custom_call" | custom-call | tf_op jit(solution)/shard_map/pallas_call | solution.py:559
  43.7 1.1 %shard_map.103 = (bf16[64,8,512]{2,1,0:T(8,128)(2,1)}, f32[4,9,32,64]{3,2,1,0:T(8,128)}, f32[32,512]{1,0:T(8,128)}, f32[1,32]{1,0:T(1,128)}) custom-call(bf16[64,8,512]{2,1,0:T(8,128)(2,1)S(1)} %get-tuple-element.13.d_ref, bf16[4,144,128]{2,1,0:T(8,128)(2,1)S(1)} %get-tuple-element.14.kg, f32[4,4,1,128]{3,2,1,0:T(1,128)S(1)} %get-tuple-element.15.st, ...), custom_call_target="tpu_custom_call" | custom-call | tf_op jit(solution)/shard_map/pallas_call | solution.py:624

commit v8 on v7

--- a/solution.py
+++ b/solution.py
@@ -331,7 +331,7 @@
 
     mine = pltpu.make_async_copy(my, quarter_of(level), mm_r.at[0])
     mine.start()
-    for d in (1, 3):
+    for d in (2, 1, 3):
         go(remote(my, quarter_of(level), mm_s.at[d], mm_r.at[d], rows=peer(d)))
 
     from_left(4, half, 1, left).wait_recv()
@@ -343,26 +343,19 @@
     send_grad(1, acc_left)
     send_grad(2, acc_right)
 
-    def passed(d, level):
-        part = quarter_of(level, slice(0, 2) if d == 1 else slice(2, 4))
-        return remote(part, part, mm_s.at[1 + d // 2 * 2 + 1], mm_r.at[1 + d // 2 * 2 + 1], rows=peer(d))
-
-    for d in (1, 3):
+
+    from_left(2, 0, most, opp).wait_recv()
+    from_right(2, half + 1, most, opp).wait_recv()
+
+    early = list(range(most)) + list(range(height + 2 - most, height + 2))
+    acc_opp = grad_rows(no_grad, opp, early)
+
+    send_block(1, left)
+    send_block(2, right)
+
+    for d in range(1, 4):
         src = lax.rem(level + 4 - d, 4)
         remote(my, quarter_of(src), mm_s.at[d], mm_r.at[d], rows=peer(4 - d)).wait_recv()
-        go(passed(d, src))
-
-    from_left(2, 0, most, opp).wait_recv()
-    from_right(2, half + 1, most, opp).wait_recv()
-
-    early = list(range(most)) + list(range(height + 2 - most, height + 2))
-    acc_opp = grad_rows(no_grad, opp, early)
-
-    send_block(1, left)
-    send_block(2, right)
-
-    for d in (1, 3):
-        passed(d, lax.rem(level + 2, 4)).wait_recv()
     mine.wait()
 
     def send_slope(i, k, shard):

time: 45 us -> 44.7 us (level)
  no operation moved by 1% of the time
where the time goes in v8:
time: 44.7 us; the launch traced here: 44.5 us
  Pallas kernels  43.9 us (98%)
  between operations  0.64 us (1%)
    pallas_call x1, Pallas kernels, on_device(): pl.pallas_call(kernel, out_shape=(jax.ShapeDtypeStruct((ch, height, width...  42.8 us
    pallas_call x1, Pallas kernels, on_device(): pl.pallas_call(write_out, out_shape=(jax.ShapeDtypeStruct((ch, height, wi...  1.09 us

profile of v8, /device:TPU:1, one launch (start us, length us, event | category | flops | bytes accessed | tf_op | source)
XLA Modules:
  0.0 44.5 jit_solution(5145337958658098657)
XLA Ops:
  0.6 42.8 %shard_map.102 = (bf16[64,8,512]{2,1,0:T(8,128)(2,1)S(1)}, bf16[4,144,128]{2,1,0:T(8,128)(2,1)S(1)}, f32[4,4,1,128]{3,2,1,0:T(1,128)S(1)}, f32[4,8,512]{2,1,0:T(8,128)S(1)}, f32[4,8,128]{2,1,0:T(8,128)S(1)}) custom-call(bf16[64,8,512]{2,1,0:T(8,128)(2,1)} %bitcast.10, bf16[64,8,512]{2,1,0:T(8,128)(2,1)} %bitcast.11, f32[4,9,32,64]{3,2,1,0:T(8,128)} %bitcast.9, ...), custom_call_target="tpu_custom_call" | custom-call | tf_op jit(solution)/shard_map/pallas_call | solution.py:552
  43.5 1.1 %shard_map.103 = (bf16[64,8,512]{2,1,0:T(8,128)(2,1)}, f32[4,9,32,64]{3,2,1,0:T(8,128)}, f32[32,512]{1,0:T(8,128)}, f32[1,32]{1,0:T(1,128)}) custom-call(bf16[64,8,512]{2,1,0:T(8,128)(2,1)S(1)} %get-tuple-element.13.d_ref, bf16[4,144,128]{2,1,0:T(8,128)(2,1)S(1)} %get-tuple-element.14.kg, f32[4,4,1,128]{3,2,1,0:T(1,128)S(1)} %get-tuple-element.15.st, ...), custom_call_target="tpu_custom_call" | custom-call | tf_op jit(solution)/shard_map/pallas_call | solution.py:617

commit v9 on v8

--- a/solution.py
+++ b/solution.py
@@ -48,8 +48,8 @@
 
 def kernel(
     x_hbm, f_hbm, bank_hbm, sel_hbm, lat_hbm, aw_hbm, ab_hbm,
-    d_ref, kg, st, latb, selb,
-    xraw, fraw, f_ref, bank_ref, sel_ref, lat_ref, aw_ref, ab_ref, xbuf, fs, fhalo, mown, ms, my, mm, mall, gs, gp, gw, gx, gk, gbuf, en, sc, slv, slo, ker_ref, plain_ref, dacc, dsend, dhalo,
+    d_ref, bg_ref, st, latb,
+    xraw, fraw, f_ref, bank_ref, sel_ref, lat_ref, aw_ref, ab_ref, xbuf, fs, fhalo, mown, ms, my, mm, mall, gs, gp, gw, gx, gk, gbuf, en, sc, slv, slo, kg, selb, ker_ref, plain_ref, dacc, dsend, dhalo,
     ag_s, ag_r, fh_s, fh_r, dh_s, dh_r, load_s, in_s, in_r, en_s, en_r, sc_s, sc_r, ms_s, ms_r, my_s, my_r, mm_s, mm_r,
     gx_s, gx_r, g_s, gf_s, g_r, sl_s, sl_r, kg_s, kg_r, st_s, st_r,
 ):
@@ -476,8 +476,19 @@
 
     for d in range(1, SAMPLES):
         src = lax.rem(b + SAMPLES - d, SAMPLES)
+        remote(kg.at[src], kg.at[src], kg_s.at[d], kg_r.at[d], samples=src).wait_recv()
+    for d in range(1, SAMPLES):
+        src = lax.rem(b + SAMPLES - d, SAMPLES)
         remote(latb.at[src], latb.at[src], in_s.at[0, d], in_r.at[0, d], samples=src).wait_recv()
         remote(selb.at[src], selb.at[src], in_s.at[1, d], in_r.at[1, d], samples=src).wait_recv()
+
+    each = [kg[s].astype(F32) for s in range(SAMPLES)]
+    for k in range(nb):
+        total = unpacked(sum(selb[s][0:1, k : k + 1] * each[s] for s in range(SAMPLES)))
+        for kw in range(3):
+            for kh in range(3):
+                bg_ref[k, 3 * kh + kw] = total[kw * ib : (kw + 1) * ib, (2 - kh) * ch : (3 - kh) * ch]
+
     for db in range(SAMPLES):
         for dc in range(CHANS):
             if db or dc:
@@ -486,10 +497,6 @@
                     st.at[bs, cs], st.at[bs, cs], st_s.at[db, dc], st_r.at[db, dc], samples=bs, chan=cs
                 ).wait_recv()
 
-    for d in range(1, SAMPLES):
-        src = lax.rem(b + SAMPLES - d, SAMPLES)
-        remote(kg.at[src], kg.at[src], kg_s.at[d], kg_r.at[d], samples=src).wait_recv()
-
     for copy in sent:
         copy.wait_send()
 
@@ -508,20 +515,15 @@
         edge(dsend.at[1], dhalo, dh_s, dh_r, False).wait_send()
 
 
-def write_out(d_ref, kg, st, latb, selb, d_hbm, bg_hbm, awg_hbm, abg_hbm, bg_ref, awg_ref, abg_ref, sems):
-    nb, _, ib, ch = bg_ref.shape
+def write_out(d_ref, bg_ref, st, latb, d_hbm, bg_hbm, awg_hbm, abg_hbm, awg_ref, abg_ref, sems):
+    nb, _, ib, _ = bg_ref.shape
     quarter = d_ref.shape[0] // 4
     copies = []
     for i in range(4):
         some = pl.ds(i * quarter, quarter)
         copies.append(pltpu.make_async_copy(d_ref.at[some], d_hbm.at[some], sems.at[2 + nb + i]))
         copies[-1].start()
-    each = [kg[s].astype(F32) for s in range(SAMPLES)]
     for k in range(nb):
-        total = unpacked(sum(selb[s][0:1, k : k + 1] * each[s] for s in range(SAMPLES)))
-        for kw in range(3):
-            for kh in range(3):
-                bg_ref[k, 3 * kh + kw] = total[kw * ib : (kw + 1) * ib, (2 - kh) * ch : (3 - kh) * ch]
         copies.append(pltpu.make_async_copy(bg_ref.at[k], bg_hbm.at[k], sems.at[2 + k]))
         copies[-1].start()
     diagonal = lax.broadcasted_iota(jnp.int32, (ib, 128), 0) == lane_iota((ib, 128))
@@ -553,13 +555,12 @@
         kernel,
         out_shape=(
             jax.ShapeDtypeStruct((ch, height, width), BF16),
-            jax.ShapeDtypeStruct((SAMPLES, 9 * ib // 2, 128), BF16),
+            jax.ShapeDtypeStruct((nb, taps, ib, ch), F32),
             jax.ShapeDtypeStruct((SAMPLES, CHANS, 1, 128), F32),
             jax.ShapeDtypeStruct((SAMPLES, 8, z), F32),
-            jax.ShapeDtypeStruct((SAMPLES, 8, 128), F32),
         ),
         in_specs=[hbm] * 7,
-        out_specs=(vmem,) * 5,
+        out_specs=(vmem,) * 4,
         scratch_shapes=[
             pltpu.VMEM((ch, height, width), BF16),
             pltpu.VMEM((ch, height, width), BF16),
@@ -587,6 +588,8 @@
             pltpu.VMEM((CHANS, 1, 128), F32),
             pltpu.VMEM((ROWS, CHANS, 1, 128), F32),
             pltpu.VMEM((CHANS, 1, 128), F32),
+            pltpu.VMEM((SAMPLES, 9 * ib // 2, 128), BF16),
+            pltpu.VMEM((SAMPLES, 8, 128), F32),
             pltpu.VMEM((3, ib, lanes), F32),
             pltpu.VMEM((3, ib, lanes), F32),
             pltpu.VMEM((height + 2, ch, width), F32),
@@ -622,10 +625,9 @@
             jax.ShapeDtypeStruct((ib, z), F32),
             jax.ShapeDtypeStruct((1, ib), F32),
         ),
-        in_specs=[vmem] * 5,
+        in_specs=[vmem] * 4,
         out_specs=(hbm,) * 4,
         scratch_shapes=[
-            pltpu.VMEM((nb, taps, ib, ch), F32),
             pltpu.VMEM((ib, z), F32),
             pltpu.VMEM((1, ib), F32),
             dma((6 + nb,)),

time: 44.7 us -> 44.7 us (level)
  no operation moved by 1% of the time
where the time goes in v9:
time: 44.7 us; the launch traced here: 44.5 us
  Pallas kernels  43.9 us (98%)
  between operations  0.64 us (1%)
    pallas_call x1, Pallas kernels, on_device(): pl.pallas_call(kernel, out_shape=(jax.ShapeDtypeStruct((ch, height, width...  42.8 us
    pallas_call x1, Pallas kernels, on_device(): pl.pallas_call(write_out, out_shape=(jax.ShapeDtypeStruct((ch, height, wi...  1.09 us

profile of v9, /device:TPU:1, one launch (start us, length us, event | category | flops | bytes accessed | tf_op | source)
XLA Modules:
  0.0 44.5 jit_solution(16791958100361202785)
XLA Ops:
  0.6 42.8 %shard_map.102 = (bf16[64,8,512]{2,1,0:T(8,128)(2,1)S(1)}, f32[4,9,32,64]{3,2,1,0:T(8,128)S(1)}, f32[4,4,1,128]{3,2,1,0:T(1,128)S(1)}, f32[4,8,512]{2,1,0:T(8,128)S(1)}) custom-call(bf16[64,8,512]{2,1,0:T(8,128)(2,1)} %bitcast.10, bf16[64,8,512]{2,1,0:T(8,128)(2,1)} %bitcast.11, f32[4,9,32,64]{3,2,1,0:T(8,128)} %bitcast.9, s32[1,4]{1,0:T(1,128)} %sel_hbm.1, ...), custom_call_target="tpu_custom_call" | custom-call | tf_op jit(solution)/shard_map/pallas_call | solution.py:554
  43.5 1.1 %shard_map.103 = (bf16[64,8,512]{2,1,0:T(8,128)(2,1)}, f32[4,9,32,64]{3,2,1,0:T(8,128)}, f32[32,512]{1,0:T(8,128)}, f32[1,32]{1,0:T(1,128)}) custom-call(bf16[64,8,512]{2,1,0:T(8,128)(2,1)S(1)} %get-tuple-element.12.d_ref, f32[4,9,32,64]{3,2,1,0:T(8,128)S(1)} %get-tuple-element.13.bg_ref, f32[4,4,1,128]{3,2,1,0:T(1,128)S(1)} %get-tuple-element.14.st, ...), custom_call_target="tpu_custom_call" | custom-call | tf_op jit(solution)/shard_map/pallas_call | solution.py:620

commit v10 on v8

--- a/solution.py
+++ b/solution.py
@@ -258,8 +258,10 @@
     def swap(i):
         return remote(gp.at[i, 1 - keep], gx.at[i], gx_s.at[i], gx_r.at[i], rows=partner)
 
-    def send_grad(i, acc):
+    def send_grad(i, acc, slope=None):
         gs[i, :, :, : 3 * ch] = acc.reshape(2, 3 * ib, 3 * ch).astype(BF16)
+        if slope:
+            send_slope(i, *slope)
         for part in range(2):
             wide = packed(acc[part * 3 * ib : (part + 1) * 3 * ib])
             gw[i, part] = wide
@@ -375,10 +377,9 @@
     from_left(3, most, 1, opp).wait_recv()
     from_right(3, half, 1, opp).wait_recv()
 
-    send_grad(3, grad_rows(acc_opp, opp, range(most, height + 2 - most)))
+    send_grad(3, grad_rows(acc_opp, opp, range(most, height + 2 - most)), slope=(2, opp))
     for part in range(2):
         go(remote(gp.at[3, part], gbuf.at[r], gf_s.at[part], g_r.at[r], rows=2 * c + part, chan=opp))
-    send_slope(3, 2, opp)
 
     for d in range(1, CHANS):
         src = lax.rem(c + CHANS - d, CHANS)

time: 44.7 us -> 44.5 us (level)
  no operation moved by 1% of the time
where the time goes in v10:
time: 44.5 us; the launch traced here: 44.3 us
  Pallas kernels  43.7 us (98%)
  between operations  0.64 us (1%)
    pallas_call x1, Pallas kernels, on_device(): pl.pallas_call(kernel, out_shape=(jax.ShapeDtypeStruct((ch, height, width...  42.6 us
    pallas_call x1, Pallas kernels, on_device(): pl.pallas_call(write_out, out_shape=(jax.ShapeDtypeStruct((ch, height, wi...  1.09 us

profile of v10, /device:TPU:1, one launch (start us, length us, event | category | flops | bytes accessed | tf_op | source)
XLA Modules:
  0.0 44.3 jit_solution(7455757043587940313)
XLA Ops:
  0.6 42.6 %shard_map.102 = (bf16[64,8,512]{2,1,0:T(8,128)(2,1)S(1)}, bf16[4,144,128]{2,1,0:T(8,128)(2,1)S(1)}, f32[4,4,1,128]{3,2,1,0:T(1,128)S(1)}, f32[4,8,512]{2,1,0:T(8,128)S(1)}, f32[4,8,128]{2,1,0:T(8,128)S(1)}) custom-call(bf16[64,8,512]{2,1,0:T(8,128)(2,1)} %bitcast.10, bf16[64,8,512]{2,1,0:T(8,128)(2,1)} %bitcast.11, f32[4,9,32,64]{3,2,1,0:T(8,128)} %bitcast.9, ...), custom_call_target="tpu_custom_call" | custom-call | tf_op jit(solution)/shard_map/pallas_call | solution.py:553
  43.2 1.1 %shard_map.103 = (bf16[64,8,512]{2,1,0:T(8,128)(2,1)}, f32[4,9,32,64]{3,2,1,0:T(8,128)}, f32[32,512]{1,0:T(8,128)}, f32[1,32]{1,0:T(1,128)}) custom-call(bf16[64,8,512]{2,1,0:T(8,128)(2,1)S(1)} %get-tuple-element.13.d_ref, bf16[4,144,128]{2,1,0:T(8,128)(2,1)S(1)} %get-tuple-element.14.kg, f32[4,4,1,128]{3,2,1,0:T(1,128)S(1)} %get-tuple-element.15.st, ...), custom_call_target="tpu_custom_call" | custom-call | tf_op jit(solution)/shard_map/pallas_call | solution.py:618
